TPU v7x, 256 devices: a whole 4x4x8 slice. The times are simulated.
256 devices in a mesh: grp: 8 (over z_lo, x), ep: 32 (over y, z_hi, core).
Axes of the slice: x: 4, y: 4, z: 8 (z_hi: 4, z_lo: 2; z = z_hi * 2 + z_lo), core: 2. Of those that a mesh axis runs over, the one named last changes fastest.
Arguments:
- tokens_one: bfloat16 [8192, 2048], P(('grp', 'ep')), may hold values from -6 to 6
- routes_one: int32 [8192, 6], P(('grp', 'ep')), may hold values from 0 to 31, all different within a row; in each aligned block of 32 rows (0 to 31, 32 to 63, ...) at most 9 rows name the same one
- gates_one: bfloat16 [8192, 6], P(('grp', 'ep')), may hold values from 0.049804688 to 0.3984375
- tokens_two: bfloat16 [8192, 2048], P(('grp', 'ep')), may hold values from -6 to 6
- routes_two: int32 [8192, 6], P(('grp', 'ep')), may hold values from 0 to 31, all different within a row; in each aligned block of 32 rows (0 to 31, 32 to 63, ...) at most 9 rows name the same one
- gates_two: bfloat16 [8192, 6], P(('grp', 'ep')), may hold values from 0.049804688 to 0.3984375
- old_table: int32 [32], replicated, may hold values from 0 to 31, each once
- new_table: int32 [32], replicated, may hold values from 0 to 31, each once
- gate_up: bfloat16 [32, 2048, 1408], P('ep'), may hold values from -0.125 to 0.125
- down_proj: bfloat16 [32, 704, 2048], P('ep'), may hold values from -0.21875 to 0.21875
- norm_gain: bfloat16 [2048], replicated, may hold values from 0.099609375 to 1.8984375
- kv_weight: bfloat16 [2048, 1024], P(None, 'grp'), may hold values from -0.125 to 0.125
Outputs:
- hidden_one: bfloat16 [8192, 2048], P(('grp', 'ep'))
- kv_one: bfloat16 [8192, 1024], P(('grp', 'ep'))
- hidden_two: bfloat16 [8192, 2048], P(('grp', 'ep'))
- kv_two: bfloat16 [8192, 1024], P(('grp', 'ep'))
- gate_up_new: bfloat16 [32, 2048, 1408], P('ep', 'grp')
- down_proj_new: bfloat16 [32, 704, 2048], P('ep', None, 'grp')
Inputs may be any that keep to these rules, and one draw needn't show every extreme that they name: `routes_one`: each row names 6 different slots; among the rows of one device no slot is named by more than 9 routes, a bound that some block reaches. `routes_two`: each row names 6 different slots; among the rows of one device no slot is named by more than 9 routes, a bound that some block reaches. `old_table`: each expert appears once. `new_table`: each expert appears once.
All inputs are finite; a program needn't handle non-finite values.
Results may differ from a plain program's by a relative error of at most 0.006.
Values may be sent and summed in bfloat16 or wider, within the bound.
A program may use at most 128 MiB of HBM per device.

v0:
```python
import jax
import jax.numpy as jnp
from jax import lax
from jax.sharding import PartitionSpec as P

TOP = 6


def expert_ffn(activation, weight_in, weight_out):
    inner = weight_out.shape[0]
    joined = jnp.dot(activation, weight_in, preferred_element_type=jnp.float32)
    gate_part = joined[:, :inner]
    upward = joined[:, inner:]
    hidden = (jax.nn.silu(gate_part) * upward).astype(jnp.bfloat16)
    return jnp.dot(hidden, weight_out, preferred_element_type=jnp.float32).astype(jnp.bfloat16)


def dispatch_plan(owners, ep_size, capacity):
    flattened = owners.reshape(-1)
    matches = (
        flattened[:, None] == lax.broadcasted_iota(jnp.int32, (flattened.shape[0], ep_size), 1)
    ).astype(jnp.int32)
    earlier = jnp.cumsum(matches, axis=0) - matches
    ranking = jnp.sum(earlier * matches, axis=1)
    return flattened * capacity + ranking


def routed_layer(tokens, owners, gate_share, weight_in, weight_out):
    ep_size = lax.axis_size("ep")
    rows_here = tokens.shape[0]
    features = tokens.shape[1]
    capacity = 3 * rows_here * TOP // (2 * ep_size)
    targets = dispatch_plan(owners, ep_size, capacity)
    senders = jnp.arange(rows_here * TOP, dtype=jnp.int32) // TOP
    packed = (
        jnp.zeros((ep_size * capacity, features), jnp.bfloat16).at[targets].set(tokens[senders])
    )
    packed = packed.reshape(ep_size, capacity, features)
    arrived = lax.all_to_all(packed, "ep", split_axis=0, concat_axis=0, tiled=True)
    sources, slot_count, columns = arrived.shape
    result = expert_ffn(arrived.reshape(sources * slot_count, columns), weight_in, weight_out)
    returned = lax.all_to_all(
        result.reshape(sources, slot_count, columns), "ep", split_axis=0, concat_axis=0, tiled=True
    )
    outputs = returned.reshape(ep_size * capacity, features)[targets].reshape(
        rows_here, TOP, features
    )
    mixture = jnp.einsum("tk,tkd->td", gate_share.astype(jnp.float32), outputs.astype(jnp.float32))
    return (tokens.astype(jnp.float32) + mixture).astype(jnp.bfloat16)


def rms_norm(hidden, norm_gain):
    values = hidden.astype(jnp.float32)
    inverse_rms = lax.rsqrt(jnp.mean(values * values, axis=-1, keepdims=True) + 1e-06)
    return (values * inverse_rms * norm_gain.astype(jnp.float32)).astype(jnp.bfloat16)


def local(
    tokens_one,
    routes_one,
    gates_one,
    tokens_two,
    routes_two,
    gates_two,
    old_table,
    new_table,
    gate_up,
    down_proj,
    norm_gain,
    kv_weight,
):
    local_in = gate_up[0]
    local_out = down_proj[0]
    ep_size = lax.axis_size("ep")
    grp_size = lax.axis_size("grp")
    numbers = jnp.arange(ep_size, dtype=jnp.int32)
    held_where = (old_table[:, None] == numbers[None, :]).astype(jnp.int32)
    old_inverse = jnp.sum(held_where * numbers[:, None], axis=0)
    wanted = (new_table[:, None] == numbers[None, :]).astype(jnp.int32)
    sources_new = jnp.sum(wanted * old_inverse[None, :], axis=1)
    features = local_in.shape[0]
    inner = local_out.shape[0]
    spread = (
        lax.all_to_all(
            local_in.reshape(ep_size, features // ep_size, 2 * inner),
            "ep",
            split_axis=0,
            concat_axis=0,
            tiled=True,
        ),
        lax.all_to_all(
            local_out.reshape(ep_size, inner // ep_size, features),
            "ep",
            split_axis=0,
            concat_axis=0,
            tiled=True,
        ),
    )
    regrouped_in = spread[0][sources_new]
    regrouped_out = spread[1][sources_new]
    collected = (
        lax.all_to_all(regrouped_in, "ep", split_axis=0, concat_axis=0, tiled=True),
        lax.all_to_all(regrouped_out, "ep", split_axis=0, concat_axis=0, tiled=True),
    )
    moved_in = collected[0].reshape(features, 2 * inner)
    moved_out = collected[1].reshape(inner, features)
    hidden_one = routed_layer(tokens_one, routes_one, gates_one, local_in, local_out)
    hidden_two = routed_layer(tokens_two, routes_two, gates_two, moved_in, moved_out)
    part_rows = features // grp_size
    part_start = lax.axis_index("grp") * part_rows
    gate_up_new = lax.dynamic_slice_in_dim(moved_in, part_start, part_rows, 0)[None]
    down_proj_new = lax.dynamic_slice_in_dim(moved_out, part_start, part_rows, 1)[None]
    normed = jnp.concatenate(
        [rms_norm(hidden_one, norm_gain), rms_norm(hidden_two, norm_gain)], axis=0
    )
    projected = jnp.dot(
        normed,
        lax.all_gather(kv_weight, "grp", axis=1, tiled=True),
        preferred_element_type=jnp.float32,
    ).astype(jnp.bfloat16)
    rows_here = tokens_one.shape[0]
    return (
        hidden_one,
        projected[:rows_here],
        hidden_two,
        projected[rows_here:],
        gate_up_new,
        down_proj_new,
    )


def solution(mesh):
    return jax.shard_map(
        local,
        mesh=mesh,
        in_specs=(
            P(("grp", "ep"), None),
            P(("grp", "ep"), None),
            P(("grp", "ep"), None),
            P(("grp", "ep"), None),
            P(("grp", "ep"), None),
            P(("grp", "ep"), None),
            P(),
            P(),
            P("ep", None, None),
            P("ep", None, None),
            P(),
            P(None, "grp"),
        ),
        out_specs=(
            P(("grp", "ep"), None),
            P(("grp", "ep"), None),
            P(("grp", "ep"), None),
            P(("grp", "ep"), None),
            P("ep", "grp", None),
            P("ep", None, "grp"),
        ),
        check_vma=False,
    )
```

profile of v0, /device:TPU:1, one launch (start us, length us, event | category | flops | bytes accessed | tf_op | source)
XLA Modules:
  0.0 724.4 jit_solution(5846512411207719492)
XLA Ops:
  9.9 5.7 scatter_custom_fusion.1
  17.2 12.9 %all-to-all-start.2 = ((bf16[32,9,2048]{2,1,0:T(8,128)(2,1)}), bf16[32,9,2048]{2,1,0:T(8,128)(2,1)S(1)}, u32[]{:S(2)}, u32[]{:S(2)}) async-start(bf16[32,9,2048]{2,1,0:T(8,128)(2,1)} %reshape.215), calls=%async_computation.2 | async-start | bytes 4194304 | tf_op jit(solution)/shard_map/all_to_all | solution.py:39
  31.5 4.6 scatter_custom_fusion
  37.7 42.4 %all-to-all-done.2 = bf16[32,9,2048]{2,1,0:T(8,128)(2,1)S(1)} async-done(((bf16[32,9,2048]{2,1,0:T(8,128)(2,1)}), bf16[32,9,2048]{2,1,0:T(8,128)(2,1)S(1)}, u32[]{:S(2)}, u32[]{:S(2)}) %all-to-all-start.2) | async-done | bytes 1179680 | tf_op jit(solution)/shard_map/all_to_all | solution.py:39
  81.4 6.1 all-to-all-start
  87.5 4.4 reshape_squeeze.7
  92.0 36.8 %all-to-all-done = bf16[32,9,2048]{2,1,0:T(8,128)(2,1)} async-done(((bf16[32,9,2048]{2,1,0:T(8,128)(2,1)}), bf16[32,9,2048]{2,1,0:T(8,128)(2,1)}, u32[]{:S(2)}, u32[]{:S(2)}) %all-to-all-start) | async-done | bytes 1179680 | tf_op jit(solution)/shard_map/all_to_all | solution.py:39
  128.8 74.1 %all_to_all.40 = bf16[32,22,2048]{2,1,0:T(8,128)(2,1)S(1)} all-to-all(bf16[32,22,2048]{2,1,0:T(8,128)(2,1)} %reshape_squeeze.7), channel_id=1, replica_groups=mesh['grp'=8,'ep'=32] {'ep'}, dimensions={0} | all-to-all | bytes 5767168 | tf_op jit(solution)/shard_map/all_to_all | solution.py:91
  202.9 19.2 %all-to-all-start.3 = ((bf16[32,64,1408]{2,1,0:T(8,128)(2,1)}), bf16[32,64,1408]{2,1,0:T(8,128)(2,1)}, u32[]{:S(2)}, u32[]{:S(2)}) async-start(bf16[32,64,1408]{2,1,0:T(8,128)(2,1)} %bitcast.68), calls=%async_computation.3 | async-start | bytes 11534336 | tf_op jit(solution)/shard_map/all_to_all | solution.py:84
  222.5 2.5 gather_fusion.2
  225.0 104.6 %all-to-all-done.3 = bf16[32,64,1408]{2,1,0:T(8,128)(2,1)} async-done(((bf16[32,64,1408]{2,1,0:T(8,128)(2,1)}), bf16[32,64,1408]{2,1,0:T(8,128)(2,1)}, u32[]{:S(2)}, u32[]{:S(2)}) %all-to-all-start.3) | async-done | bytes 5767200 | tf_op jit(solution)/shard_map/all_to_all | solution.py:84
  329.5 27.4 %all-to-all-start.6 = ((bf16[32,22,2048]{2,1,0:T(8,128)(2,1)}), bf16[32,22,2048]{2,1,0:T(8,128)(2,1)S(1)}, u32[]{:S(2)}, u32[]{:S(2)}) async-start(bf16[32,22,2048]{2,1,0:T(8,128)(2,1)} %gather_fusion.2), calls=%async_computation.6 | async-start | bytes 6291456 | tf_op jit(solution)/shard_map/all_to_all | solution.py:103
  357.0 6.4 gather_fusion.1
  363.3 55.6 %all-to-all-done.6 = bf16[32,22,2048]{2,1,0:T(8,128)(2,1)S(1)} async-done(((bf16[32,22,2048]{2,1,0:T(8,128)(2,1)}), bf16[32,22,2048]{2,1,0:T(8,128)(2,1)S(1)}, u32[]{:S(2)}, u32[]{:S(2)}) %all-to-all-start.6) | async-done | bytes 2883616 | tf_op jit(solution)/shard_map/all_to_all | solution.py:103
  418.9 17.0 %all-to-all-start.4 = ((bf16[32,64,1408]{2,1,0:T(8,128)(2,1)}), bf16[32,64,1408]{2,1,0:T(8,128)(2,1)}, u32[]{:S(2)}, u32[]{:S(2)}) async-start(bf16[32,64,1408]{2,1,0:T(8,128)(2,1)} %gather_fusion.1), calls=%async_computation.4 | async-start | bytes 11534336 | tf_op jit(solution)/shard_map/all_to_all | solution.py:102
  436.6 2.6 reshape.209
  439.3 5.1 fusion
  444.4 2.2 fusion.4
  446.6 2.7 reshape.210
  449.2 156.3 %all-to-all-done.4 = bf16[32,64,1408]{2,1,0:T(8,128)(2,1)} async-done(((bf16[32,64,1408]{2,1,0:T(8,128)(2,1)}), bf16[32,64,1408]{2,1,0:T(8,128)(2,1)}, u32[]{:S(2)}, u32[]{:S(2)}) %all-to-all-start.4) | async-done | bytes 5767200 | tf_op jit(solution)/shard_map/all_to_all | solution.py:102
  605.5 6.1 all-to-all-start.1
  611.6 2.6 reshape.216
  614.3 2.4 reshape.218
  616.7 5.1 fusion.42
  624.6 27.4 %all-to-all-done.1 = bf16[32,9,2048]{2,1,0:T(8,128)(2,1)} async-done(((bf16[32,9,2048]{2,1,0:T(8,128)(2,1)}), bf16[32,9,2048]{2,1,0:T(8,128)(2,1)}, u32[]{:S(2)}, u32[]{:S(2)}) %all-to-all-start.1) | async-done | bytes 1179680 | tf_op jit(solution)/shard_map/all_to_all | solution.py:42
  652.0 15.4 %all-to-all-start.7 = ((bf16[32,9,2048]{2,1,0:T(8,128)(2,1)}), bf16[32,9,2048]{2,1,0:T(8,128)(2,1)S(1)}, u32[]{:S(2)}, u32[]{:S(2)}) async-start(bf16[32,9,2048]{2,1,0:T(8,128)(2,1)} %reshape.219), calls=%async_computation.7 | async-start | bytes 4194304 | tf_op jit(solution)/shard_map/all_to_all | solution.py:42
  668.9 1.8 reshape.211
  670.7 2.1 gather_fusion
  675.3 1.8 dynamic-slice_bitcast_fusion.1
  677.1 2.0 dynamic-slice_bitcast_fusion
  679.1 31.5 %all-to-all-done.7 = bf16[32,9,2048]{2,1,0:T(8,128)(2,1)S(1)} async-done(((bf16[32,9,2048]{2,1,0:T(8,128)(2,1)}), bf16[32,9,2048]{2,1,0:T(8,128)(2,1)S(1)}, u32[]{:S(2)}, u32[]{:S(2)}) %all-to-all-start.7) | async-done | bytes 1179680 | tf_op jit(solution)/shard_map/all_to_all | solution.py:42
  713.8 3.0 convolution_convert_fusion.1
  (87 shorter events, 20.0 us)
Async XLA Ops:
  17.2 12.9 %copy-start.8 = (s32[32,6]{0,1:T(8,128)S(1)}, s32[32,6]{0,1:T(8,128)}, u32[]{:S(2)}) copy-start(s32[32,6]{0,1:T(8,128)} %param.13) | copy-start | bytes 2308
  17.2 14.3 %copy-start.5 = (bf16[32,2048]{1,0:T(8,128)(2,1)S(1)}, bf16[32,2048]{1,0:T(8,128)(2,1)}, u32[]{:S(2)}) copy-start(bf16[32,2048]{1,0:T(8,128)(2,1)} %param.12) | copy-start | bytes 393220
  17.2 62.9 %all-to-all-start.2 = ((bf16[32,9,2048]{2,1,0:T(8,128)(2,1)}), bf16[32,9,2048]{2,1,0:T(8,128)(2,1)S(1)}, u32[]{:S(2)}, u32[]{:S(2)}) async-start(bf16[32,9,2048]{2,1,0:T(8,128)(2,1)} %reshape.215), calls=%async_computation.2 | async-start | bytes 4194304 | tf_op jit(solution)/shard_map/all_to_all | solution.py:39
  80.1 1.3 copy-start
  81.4 47.4 %all-to-all-start = ((bf16[32,9,2048]{2,1,0:T(8,128)(2,1)}), bf16[32,9,2048]{2,1,0:T(8,128)(2,1)}, u32[]{:S(2)}, u32[]{:S(2)}) async-start(bf16[32,9,2048]{2,1,0:T(8,128)(2,1)} %reshape.208), calls=%async_computation | async-start | bytes 4194304 | tf_op jit(solution)/shard_map/all_to_all | solution.py:39
  202.9 19.3 %copy-start.13 = (s32[32]{0:T(128)S(1)}, s32[32]{0:T(128)}, u32[]{:S(2)}) copy-start(s32[32]{0:T(128)} %param.18) | copy-start | bytes 388
  202.9 19.4 %copy-start.14 = (s32[32]{0:T(128)S(1)}, s32[32]{0:T(128)}, u32[]{:S(2)}) copy-start(s32[32]{0:T(128)} %param.19) | copy-start | bytes 388
  202.9 126.6 %all-to-all-start.3 = ((bf16[32,64,1408]{2,1,0:T(8,128)(2,1)}), bf16[32,64,1408]{2,1,0:T(8,128)(2,1)}, u32[]{:S(2)}, u32[]{:S(2)}) async-start(bf16[32,64,1408]{2,1,0:T(8,128)(2,1)} %bitcast.68), calls=%async_computation.3 | async-start | bytes 11534336 | tf_op jit(solution)/shard_map/all_to_all | solution.py:84
  329.5 89.3 %all-to-all-start.6 = ((bf16[32,22,2048]{2,1,0:T(8,128)(2,1)}), bf16[32,22,2048]{2,1,0:T(8,128)(2,1)S(1)}, u32[]{:S(2)}, u32[]{:S(2)}) async-start(bf16[32,22,2048]{2,1,0:T(8,128)(2,1)} %gather_fusion.2), calls=%async_computation.6 | async-start | bytes 6291456 | tf_op jit(solution)/shard_map/all_to_all | solution.py:103
  418.9 186.6 %all-to-all-start.4 = ((bf16[32,64,1408]{2,1,0:T(8,128)(2,1)}), bf16[32,64,1408]{2,1,0:T(8,128)(2,1)}, u32[]{:S(2)}, u32[]{:S(2)}) async-start(bf16[32,64,1408]{2,1,0:T(8,128)(2,1)} %gather_fusion.1), calls=%async_computation.4 | async-start | bytes 11534336 | tf_op jit(solution)/shard_map/all_to_all | solution.py:102
  435.9 277.9 %all-gather.2.cloned.1.call-start = ((), (), s32[]{:S(2)}) async-start(), calls=%async_computation.8 | async-start | bytes 4718592 | tf_op jit(solution)/shard_map/all_gather | solution.py:118
  439.3 5.1 copy-start.2
  605.5 46.5 %all-to-all-start.1 = ((bf16[32,9,2048]{2,1,0:T(8,128)(2,1)}), bf16[32,9,2048]{2,1,0:T(8,128)(2,1)}, u32[]{:S(2)}, u32[]{:S(2)}) async-start(bf16[32,9,2048]{2,1,0:T(8,128)(2,1)} %reshape.210), calls=%async_computation.1 | async-start | bytes 4194304 | tf_op jit(solution)/shard_map/all_to_all | solution.py:42
  616.7 5.1 copy-start.1
  624.6 42.8 %copy-start.11 = (bf16[32,6]{0,1:T(8,128)(2,1)S(1)}, bf16[32,6]{0,1:T(8,128)(2,1)}, u32[]{:S(2)}) copy-start(bf16[32,6]{0,1:T(8,128)(2,1)} %param.17) | copy-start | bytes 1156
  624.6 43.0 %copy-start.12 = (bf16[32,6]{0,1:T(8,128)(2,1)S(1)}, bf16[32,6]{0,1:T(8,128)(2,1)}, u32[]{:S(2)}) copy-start(bf16[32,6]{0,1:T(8,128)(2,1)} %param.14) | copy-start | bytes 1156
  624.6 43.1 %copy-start.9 = (bf16[2048]{0:T(1024)(128)(2,1)S(1)}, bf16[2048]{0:T(1024)(128)(2,1)}, u32[]{:S(2)}) copy-start(bf16[2048]{0:T(1024)(128)(2,1)} %param.22) | copy-start | bytes 12292
  652.0 58.7 %all-to-all-start.7 = ((bf16[32,9,2048]{2,1,0:T(8,128)(2,1)}), bf16[32,9,2048]{2,1,0:T(8,128)(2,1)S(1)}, u32[]{:S(2)}, u32[]{:S(2)}) async-start(bf16[32,9,2048]{2,1,0:T(8,128)(2,1)} %reshape.219), calls=%async_computation.7 | async-start | bytes 4194304 | tf_op jit(solution)/shard_map/all_to_all | solution.py:42
  675.3 38.3 %copy-start.3 = (bf16[32,2048]{1,0:T(8,128)(2,1)}, bf16[32,2048]{1,0:T(8,128)(2,1)S(1)}, u32[]{:S(2)}) copy-start(bf16[32,2048]{1,0:T(8,128)(2,1)S(1)} %get-tuple-element.7) | copy-start | bytes 393220
  712.5 0.9 copy-start.6
  712.5 1.1 copy-start.10
  712.5 1.1 copy-start.7
  713.6 3.3 copy-start.4
Sparse Core Ops, SparseCore 0:
  438.5 142.8 all-gather.1
where the time goes:
time: 733 us; the launch traced here: 724 us
  waiting for transfers between devices  455 us (62%)
  starting transfers between devices  104 us (14%)
  blocking collectives  74.1 us (10%)
  local copies, waits for them, and re-layouts  54.1 us (7%)
  matrix products  17.5 us (2%)
  between operations  14.4 us (2%)
    all_to_all x1, waiting for transfers between devices, local(): lax.all_to_all(regrouped_in, 'ep', split_axis=0, concat_axis=0, tiled=True)  156 us
    all_to_all x1, waiting for transfers between devices, local(): lax.all_to_all(local_in.reshape(ep_size, features // ep_size, 2 * inner),...  105 us
    all_to_all x2, waiting for transfers between devices, routed_layer(): lax.all_to_all(packed, 'ep', split_axis=0, concat_axis=0, tiled=True)  79.2 us
    all_to_all x1, blocking collectives, local(): lax.all_to_all(local_out.reshape(ep_size, inner // ep_size, features), 'e...  74.1 us
    all_to_all x2, waiting for transfers between devices, routed_layer(): lax.all_to_all(result.reshape(sources, slot_count, columns), 'ep', split_...  58.9 us
    all_to_all x1, waiting for transfers between devices, local(): lax.all_to_all(regrouped_out, 'ep', split_axis=0, concat_axis=0, tiled=True)  55.6 us
    all_to_all x1, starting transfers between devices, local(): lax.all_to_all(regrouped_out, 'ep', split_axis=0, concat_axis=0, tiled=True)  27.4 us
    all_to_all x2, starting transfers between devices, routed_layer(): lax.all_to_all(result.reshape(sources, slot_count, columns), 'ep', split_...  21.6 us
  transfers between devices with their start and end apart: 8, of which 7 were waited for; matrix products, arithmetic and copies ran while one was open for 8% of the time, Pallas kernels for 0%

commit v1 on v0

v1 whole, which is shorter than its diff:
```python
import jax
import jax.numpy as jnp
from jax import lax
from jax.sharding import PartitionSpec as P

TOP = 6


def slot_table(owners, ep_size, offset):
    rows = owners.shape[0]
    hits = (owners[:, :, None] == jnp.arange(ep_size, dtype=jnp.int32)[None, None, :])
    named = jnp.any(hits, axis=1)
    lower = jnp.tril(jnp.ones((rows, rows), jnp.float32), -1)
    rank = jnp.dot(lower, named.astype(jnp.float32), preferred_element_type=jnp.float32)
    return jnp.where(named, rank.astype(jnp.int32) + offset, -1), hits


def gate_table(hits, gates):
    return jnp.sum(jnp.where(hits, gates.astype(jnp.float32)[:, :, None], 0.0), axis=1)


def local(
    tokens_one,
    routes_one,
    gates_one,
    tokens_two,
    routes_two,
    gates_two,
    old_table,
    new_table,
    gate_up,
    down_proj,
    norm_gain,
    kv_weight,
):
    weight_in = gate_up[0]
    weight_out = down_proj[0]
    ep_size = lax.axis_size("ep")
    grp_size = lax.axis_size("grp")
    numbers = jnp.arange(ep_size, dtype=jnp.int32)
    old_inverse = jnp.sum((old_table[:, None] == numbers[None, :]).astype(jnp.int32) * numbers[:, None], axis=0)
    wanted = (new_table[:, None] == numbers[None, :]).astype(jnp.int32)
    sources_new = jnp.sum(wanted * old_inverse[None, :], axis=1)
    features, inner = weight_in.shape[0], weight_out.shape[0]
    part = features // grp_size
    start = lax.axis_index("grp") * part
    piece_in = lax.dynamic_slice_in_dim(weight_in, start, part, 0)
    piece_out = lax.dynamic_slice_in_dim(weight_out, start, part, 1)
    n_in, n_out = piece_in.size // ep_size, piece_out.size // ep_size
    pieces = jnp.concatenate(
        [piece_in.reshape(ep_size, n_in // 128, 128), piece_out.reshape(ep_size, n_out // 128, 128)], axis=1
    )
    spread = lax.all_to_all(pieces, "ep", split_axis=0, concat_axis=0, tiled=True)

    rows = tokens_one.shape[0]
    capacity = 3 * rows * TOP // (2 * ep_size)
    owners_two = jnp.sum(
        (routes_two[:, :, None] == numbers[None, None, :]).astype(jnp.int32) * sources_new[None, None, :], axis=2
    )
    table_one, hits_one = slot_table(routes_one, ep_size, 0)
    table_two, hits_two = slot_table(owners_two, ep_size, capacity)
    table = jnp.concatenate([table_one, table_two], axis=0)
    gates = jnp.concatenate([gate_table(hits_one, gates_one), gate_table(hits_two, gates_two)], axis=0)
    tokens = jnp.concatenate([tokens_one, tokens_two], axis=0)
    both = 2 * rows
    slots = jnp.arange(2 * capacity, dtype=jnp.int32)
    chosen = table[:, :, None] == slots[None, None, :]
    pick = chosen.astype(jnp.bfloat16).reshape(both, ep_size * 2 * capacity)
    mix = jnp.where(chosen, gates[:, :, None], 0.0).astype(jnp.bfloat16).reshape(both, ep_size * 2 * capacity)
    packed = lax.dot_general(
        pick, tokens, (((0,), (0,)), ((), ())), preferred_element_type=jnp.float32
    ).astype(jnp.bfloat16)
    arrived = lax.all_to_all(
        packed.reshape(ep_size, 2 * capacity, features), "ep", split_axis=0, concat_axis=0, tiled=True
    )
    activation = arrived.reshape(ep_size * 2 * capacity, features)
    joined = jnp.dot(activation, weight_in, preferred_element_type=jnp.float32)
    hidden = (jax.nn.silu(joined[:, :inner]) * joined[:, inner:]).astype(jnp.bfloat16)
    result = jnp.dot(hidden, weight_out, preferred_element_type=jnp.float32).astype(jnp.bfloat16)
    returned = lax.all_to_all(
        result.reshape(ep_size, 2 * capacity, features), "ep", split_axis=0, concat_axis=0, tiled=True
    ).reshape(ep_size * 2 * capacity, features)
    collected = lax.all_to_all(spread[sources_new], "ep", split_axis=0, concat_axis=0, tiled=True)
    cut = n_in // 128
    gate_up_new = collected[:, :cut].reshape(1, part, 2 * inner)
    down_proj_new = collected[:, cut:].reshape(1, inner, part)
    mixture = jnp.dot(mix, returned, preferred_element_type=jnp.float32)
    out = (tokens.astype(jnp.float32) + mixture).astype(jnp.bfloat16)
    values = out.astype(jnp.float32)
    inverse_rms = lax.rsqrt(jnp.mean(values * values, axis=-1, keepdims=True) + 1e-06)
    normed = (values * inverse_rms * norm_gain.astype(jnp.float32)).astype(jnp.bfloat16)
    projected = jnp.dot(
        normed,
        lax.all_gather(kv_weight, "grp", axis=1, tiled=True),
        preferred_element_type=jnp.float32,
    ).astype(jnp.bfloat16)
    return (out[:rows], projected[:rows], out[rows:], projected[rows:], gate_up_new, down_proj_new)


def solution(mesh):
    split = P(("grp", "ep"), None)
    return jax.shard_map(
        local,
        mesh=mesh,
        in_specs=(split,) * 6 + (P(), P(), P("ep", None, None), P("ep", None, None), P(), P(None, "grp")),
        out_specs=(split,) * 4 + (P("ep", "grp", None), P("ep", None, "grp")),
        check_vma=False,
    )
```

time: 733 us -> 301 us (0.41); the launches traced: 724 us -> 300 us
  waiting for transfers between devices: 455 us -> 199 us
  starting transfers between devices: 104 us -> 29.5 us
  blocking collectives: 74.1 us -> 0 us
  local copies, waits for them, and re-layouts: 54.1 us -> 34.5 us
    all_to_all x7 -> x4, waiting for transfers between devices: 455 us -> 198 us  [the longest x1 91.4 us: local(): lax.all_to_all(result.reshape(ep_size, 2 * capacity, features), 'ep', spl...]
    all_to_all x7 -> x4, starting transfers between devices: 104 us -> 29.5 us  [the longest x1 12.8 us: local(): lax.all_to_all(pieces, 'ep', split_axis=0, concat_axis=0, tiled=True)]
    all_to_all x1 -> x0, blocking collectives: 74.1 us -> none  [local(): lax.all_to_all(local_out.reshape(ep_size, inner // ep_size, features), 'e...]
    scatter x2 -> x0, local copies, waits for them, and re-layouts: 10.3 us -> none  [routed_layer(): jnp.zeros((ep_size * capacity, features), jnp.bfloat16).at[targets]]
    gather x4 -> x1, local copies, waits for them, and re-layouts: 12.2 us -> 2.96 us  [local(): spread[sources_new]]
    reshape x11 -> x7, local copies, waits for them, and re-layouts: 19.1 us -> 21.2 us  [the longest x1 4.34 us: local(): activation = arrived.reshape(ep_size * 2 * capacity, features)]
  transfers between devices with their start and end apart: 8 -> 5, of which waited for: 7 -> 4; matrix products, arithmetic and copies ran while one was open for 8% -> 15% of each run, Pallas kernels for 0% -> 0%
where the time goes in v1:
time: 301 us; the launch traced here: 300 us
  waiting for transfers between devices  199 us (66%)
  local copies, waits for them, and re-layouts  34.5 us (11%)
  starting transfers between devices  29.5 us (10%)
  matrix products  19.8 us (7%)
  between operations  14.4 us (5%)
  other arithmetic  3.32 us (1%)
    all_to_all x1, waiting for transfers between devices, local(): lax.all_to_all(result.reshape(ep_size, 2 * capacity, features), 'ep', spl...  91.4 us
    all_to_all x1, waiting for transfers between devices, local(): lax.all_to_all(packed.reshape(ep_size, 2 * capacity, features), 'ep', spl...  71.6 us
    all_to_all x1, waiting for transfers between devices, local(): lax.all_to_all(pieces, 'ep', split_axis=0, concat_axis=0, tiled=True)  18.4 us
    all_to_all x1, waiting for transfers between devices, local(): lax.all_to_all(spread[sources_new], 'ep', split_axis=0, concat_axis=0, ti...  16.5 us
    all_to_all x1, starting transfers between devices, local(): lax.all_to_all(pieces, 'ep', split_axis=0, concat_axis=0, tiled=True)  12.8 us
    all_to_all x1, starting transfers between devices, local(): lax.all_to_all(packed.reshape(ep_size, 2 * capacity, features), 'ep', spl...  7.28 us
    dot_general x1, matrix products, local(): joined = jnp.dot(activation, weight_in, preferred_element_type=jnp.float32)  6.89 us
  transfers between devices with their start and end apart: 5, of which 4 were waited for; matrix products, arithmetic and copies ran while one was open for 15% of the time, Pallas kernels for 0%

profile of v1, /device:TPU:1, one launch (start us, length us, event | category | flops | bytes accessed | tf_op | source)
XLA Modules:
  0.0 300.1 jit_solution(16771781120365309865)
XLA Ops:
  7.2 2.2 constant_dynamic-slice_fusion.1
  9.4 2.6 reshape.78
  12.0 0.8 constant_dynamic-slice_fusion
  12.8 1.1 reshape.79
  14.0 2.3 pad_maximum_fusion
  16.3 12.8 %all-to-all-start.2 = ((bf16[32,132,128]{2,1,0:T(8,128)(2,1)}), bf16[32,132,128]{2,1,0:T(8,128)(2,1)}, u32[]{:S(2)}, u32[]{:S(2)}) async-start(bf16[32,132,128]{2,1,0:T(8,128)(2,1)} %pad_maximum_fusion), calls=%async_computation.2 | async-start | bytes 2228224 | tf_op jit(solution)/shard_map/all_to_all | solution.py:53
  29.4 0.3 select_reduce_fusion.2
  30.6 0.7 eq.107
  31.4 0.9 constant_dynamic-update-slice_fusion
  32.4 3.2 %convolution_convert_fusion.1 = bf16[576,2048]{1,0:T(8,128)(2,1)} fusion(bf16[64,2048]{1,0:T(8,128)(2,1)S(1)} %constant_dynamic-update-slice_fusion, s32[64,576]{0,1:T(8,128)} %eq.107, s32[576]{0:T(1024)S(1)} %eq.109), kind=kOutput, calls=%fused_computation.4 | convolution fusion | flops 152211456 | bytes 2771200 | tf_op jit(solution)/shard_map/dot_general | solution.py:70
  35.6 4.3 %reshape.75 = bf16[32,18,2048]{2,1,0:T(8,128)(2,1)} reshape(bf16[576,2048]{1,0:T(8,128)(2,1)} %convolution_convert_fusion.1) | data formatting | bytes 4718592 | tf_op jit(solution)/shard_map/reshape | solution.py:74
  39.9 18.4 %all-to-all-done.2 = bf16[32,132,128]{2,1,0:T(8,128)(2,1)} async-done(((bf16[32,132,128]{2,1,0:T(8,128)(2,1)}), bf16[32,132,128]{2,1,0:T(8,128)(2,1)}, u32[]{:S(2)}, u32[]{:S(2)}) %all-to-all-start.2) | async-done | bytes 1081376 | tf_op jit(solution)/shard_map/all_to_all | solution.py:53
  58.3 7.3 %all-to-all-start = ((bf16[32,18,2048]{2,1,0:T(8,128)(2,1)}), bf16[32,18,2048]{2,1,0:T(8,128)(2,1)}, u32[]{:S(2)}, u32[]{:S(2)}) async-start(bf16[32,18,2048]{2,1,0:T(8,128)(2,1)} %reshape.75), calls=%async_computation | async-start | bytes 6291456 | tf_op jit(solution)/shard_map/all_to_all | solution.py:73
  65.6 3.0 gather_fusion
  68.6 71.6 %all-to-all-done = bf16[32,18,2048]{2,1,0:T(8,128)(2,1)} async-done(((bf16[32,18,2048]{2,1,0:T(8,128)(2,1)}), bf16[32,18,2048]{2,1,0:T(8,128)(2,1)}, u32[]{:S(2)}, u32[]{:S(2)}) %all-to-all-start) | async-done | bytes 2359328 | tf_op jit(solution)/shard_map/all_to_all | solution.py:73
  140.1 4.7 %all-to-all-start.3 = ((bf16[32,132,128]{2,1,0:T(8,128)(2,1)}), bf16[32,132,128]{2,1,0:T(8,128)(2,1)}, u32[]{:S(2)}, u32[]{:S(2)}) async-start(bf16[32,132,128]{2,1,0:T(8,128)(2,1)} %gather_fusion), calls=%async_computation.3 | async-start | bytes 2228224 | tf_op jit(solution)/shard_map/all_to_all | solution.py:83
  144.9 0.7 all-gather.2.cloned.1.call-update
  145.6 4.3 %reshape.76 = bf16[576,2048]{1,0:T(8,128)(2,1)} reshape(bf16[32,18,2048]{2,1,0:T(8,128)(2,1)} %all-to-all-done) | data formatting | bytes 4718592 | tf_op jit(solution)/shard_map/reshape | solution.py:76
  150.0 6.9 %fusion = f32[576,1408]{1,0:T(8,128)S(1)} fusion(bf16[576,2048]{1,0:T(8,128)(2,1)} %reshape.76, bf16[1,2048,1408]{2,1,0:T(8,128)(2,1)} %param.20), kind=kOutput, calls=%fused_computation.1 | convolution fusion | flops 3321888768 | bytes 11370496 | tf_op jit(solution)/shard_map/dot_general | solution.py:77
  156.9 3.6 %convolution_convert_fusion = bf16[576,2048]{1,0:T(8,128)(2,1)} fusion(bf16[1,704,2048]{2,1,0:T(8,128)(2,1)S(1)} %copy-done, f32[576,1408]{1,0:T(8,128)S(1)} %fusion), kind=kOutput, calls=%fused_computation.3 | convolution fusion | flops 1664557056 | bytes 8781824 | tf_op jit(solution)/shard_map/dot_general | solution.py:79
  160.4 4.3 %reshape.77 = bf16[32,18,2048]{2,1,0:T(8,128)(2,1)} reshape(bf16[576,2048]{1,0:T(8,128)(2,1)} %convolution_convert_fusion) | data formatting | bytes 4718592 | tf_op jit(solution)/shard_map/reshape | solution.py:81
  164.8 16.5 %all-to-all-done.3 = bf16[32,132,128]{2,1,0:T(8,128)(2,1)} async-done(((bf16[32,132,128]{2,1,0:T(8,128)(2,1)}), bf16[32,132,128]{2,1,0:T(8,128)(2,1)}, u32[]{:S(2)}, u32[]{:S(2)}) %all-to-all-start.3) | async-done | bytes 1081376 | tf_op jit(solution)/shard_map/all_to_all | solution.py:83
  181.3 4.7 %all-to-all-start.1 = ((bf16[32,18,2048]{2,1,0:T(8,128)(2,1)}), bf16[32,18,2048]{2,1,0:T(8,128)(2,1)}, u32[]{:S(2)}, u32[]{:S(2)}) async-start(bf16[32,18,2048]{2,1,0:T(8,128)(2,1)} %reshape.77), calls=%async_computation.1 | async-start | bytes 6291456 | tf_op jit(solution)/shard_map/all_to_all | solution.py:80
  186.4 2.0 slice.40
  188.4 2.6 reshape.80
  191.1 1.8 slice.41
  192.8 1.9 reshape.81
  194.7 91.4 %all-to-all-done.1 = bf16[32,18,2048]{2,1,0:T(8,128)(2,1)} async-done(((bf16[32,18,2048]{2,1,0:T(8,128)(2,1)}), bf16[32,18,2048]{2,1,0:T(8,128)(2,1)}, u32[]{:S(2)}, u32[]{:S(2)}) %all-to-all-start.1) | async-done | bytes 2359328 | tf_op jit(solution)/shard_map/all_to_all | solution.py:80
  286.1 2.7 fusion.11
  288.8 0.7 fusion.39
  289.5 3.1 %convolution_convert_fusion.2 = bf16[64,1024]{1,0:T(8,128)(2,1)S(1)} fusion(bf16[2048,1024]{1,0:T(8,128)(2,1)} %all-gather.2.cloned.1.call-done, bf16[64,2048]{1,0:T(8,128)(2,1)S(1)} %get-tuple-element.11, f32[2048]{0:T(1024)S(1)} %convert_element_type.59, f32[64]{0:T(128)S(1)} %add_rsqrt_fusion), kind=kOutput, calls=%fused_computation.11 | convolution fusion | flops 269025280 | bytes 4595968 | tf_op jit(solution)/shard_map/dot_general | solution.py:92
  292.6 0.7 fusion.40
  (54 shorter events, 1.7 us)
Async XLA Ops:
  7.2 4.8 %copy-start = (bf16[1,704,2048]{2,1,0:T(8,128)(2,1)S(1)}, bf16[1,704,2048]{2,1,0:T(8,128)(2,1)}, u32[]{:S(2)}) copy-start(bf16[1,704,2048]{2,1,0:T(8,128)(2,1)} %param.21) | copy-start | bytes 8650756
  13.9 15.1 %copy-start.12 = (s32[32]{0:T(128)S(1)}, s32[32]{0:T(128)}, u32[]{:S(2)}) copy-start(s32[32]{0:T(128)} %param.18) | copy-start | bytes 388
  13.9 15.2 %copy-start.13 = (s32[32]{0:T(128)S(1)}, s32[32]{0:T(128)}, u32[]{:S(2)}) copy-start(s32[32]{0:T(128)} %param.19) | copy-start | bytes 388
  14.0 15.4 %copy-start.7 = (s32[32,6]{0,1:T(8,128)S(1)}, s32[32,6]{0,1:T(8,128)}, u32[]{:S(2)}) copy-start(s32[32,6]{0,1:T(8,128)} %param.16) | copy-start | bytes 2308
  14.0 15.9 %copy-start.4 = (s32[32,6]{0,1:T(8,128)S(1)}, s32[32,6]{0,1:T(8,128)}, u32[]{:S(2)}) copy-start(s32[32,6]{0,1:T(8,128)} %param.13) | copy-start | bytes 2308
  14.0 17.4 %copy-start.1 = (bf16[32,2048]{1,0:T(8,128)(2,1)S(1)}, bf16[32,2048]{1,0:T(8,128)(2,1)}, u32[]{:S(2)}) copy-start(bf16[32,2048]{1,0:T(8,128)(2,1)} %param.12) | copy-start | bytes 393220
  16.3 42.0 %all-to-all-start.2 = ((bf16[32,132,128]{2,1,0:T(8,128)(2,1)}), bf16[32,132,128]{2,1,0:T(8,128)(2,1)}, u32[]{:S(2)}, u32[]{:S(2)}) async-start(bf16[32,132,128]{2,1,0:T(8,128)(2,1)} %pad_maximum_fusion), calls=%async_computation.2 | async-start | bytes 2228224 | tf_op jit(solution)/shard_map/all_to_all | solution.py:53
  29.4 2.0 copy-start.10
  29.6 0.8 copy-start.2
  39.9 25.7 %copy-start.11 = (s32[32]{0:T(128)S(1)}, s32[32]{0:T(128)}, u32[]{:S(2)}) copy-start(s32[32]{0:T(128)} %copy-done.10) | copy-start | bytes 388
  58.3 81.8 %all-to-all-start = ((bf16[32,18,2048]{2,1,0:T(8,128)(2,1)}), bf16[32,18,2048]{2,1,0:T(8,128)(2,1)}, u32[]{:S(2)}, u32[]{:S(2)}) async-start(bf16[32,18,2048]{2,1,0:T(8,128)(2,1)} %reshape.75), calls=%async_computation | async-start | bytes 6291456 | tf_op jit(solution)/shard_map/all_to_all | solution.py:73
  140.1 41.2 %all-to-all-start.3 = ((bf16[32,132,128]{2,1,0:T(8,128)(2,1)}), bf16[32,132,128]{2,1,0:T(8,128)(2,1)}, u32[]{:S(2)}, u32[]{:S(2)}) async-start(bf16[32,132,128]{2,1,0:T(8,128)(2,1)} %gather_fusion), calls=%async_computation.3 | async-start | bytes 2228224 | tf_op jit(solution)/shard_map/all_to_all | solution.py:83
  144.9 144.7 %all-gather.2.cloned.1.call-start = ((), (), s32[]{:S(2)}) async-start(), calls=%async_computation.4 | async-start | bytes 4718592 | tf_op jit(solution)/shard_map/all_gather | solution.py:94
  164.8 21.2 %copy-start.8 = (bf16[32,6]{0,1:T(8,128)(2,1)S(1)}, bf16[32,6]{0,1:T(8,128)(2,1)}, u32[]{:S(2)}) copy-start(bf16[32,6]{0,1:T(8,128)(2,1)} %param.17) | copy-start | bytes 1156
  164.8 21.2 %copy-start.9 = (bf16[32,6]{0,1:T(8,128)(2,1)S(1)}, bf16[32,6]{0,1:T(8,128)(2,1)}, u32[]{:S(2)}) copy-start(bf16[32,6]{0,1:T(8,128)(2,1)} %param.14) | copy-start | bytes 1156
  164.8 21.3 %copy-start.3 = (s32[32,6]{0,1:T(8,128)S(1)}, s32[32,6]{0,1:T(8,128)}, u32[]{:S(2)}) copy-start(s32[32,6]{0,1:T(8,128)} %copy-done.2) | copy-start | bytes 2308
  164.8 21.4 %copy-start.5 = (s32[32,6]{0,1:T(8,128)S(1)}, s32[32,6]{0,1:T(8,128)}, u32[]{:S(2)}) copy-start(s32[32,6]{0,1:T(8,128)} %param.13) | copy-start | bytes 2308
  164.8 21.6 %copy-start.6 = (bf16[2048]{0:T(1024)(128)(2,1)S(1)}, bf16[2048]{0:T(1024)(128)(2,1)}, u32[]{:S(2)}) copy-start(bf16[2048]{0:T(1024)(128)(2,1)} %param.22) | copy-start | bytes 12292
  181.3 104.8 %all-to-all-start.1 = ((bf16[32,18,2048]{2,1,0:T(8,128)(2,1)}), bf16[32,18,2048]{2,1,0:T(8,128)(2,1)}, u32[]{:S(2)}, u32[]{:S(2)}) async-start(bf16[32,18,2048]{2,1,0:T(8,128)(2,1)} %reshape.77), calls=%async_computation.1 | async-start | bytes 6291456 | tf_op jit(solution)/shard_map/all_to_all | solution.py:80
Sparse Core Ops, SparseCore 0:
  147.4 120.8 all-gather.1

commit v2 on v1

v2 whole, which is shorter than its diff:
```python
import jax
import jax.numpy as jnp
from jax import lax
from jax.experimental import pallas as pl
from jax.experimental.pallas import tpu as pltpu
from jax.sharding import PartitionSpec as P

TOP = 6
CHUNKS = 4
BF, F32 = jnp.bfloat16, jnp.float32
MESH = pl.DeviceIdType.MESH


def above(values, step, count):
    total = jnp.zeros_like(values)
    for i in range(1, count):
        total = total + (values >= i * step).astype(jnp.int32)
    return total


def iota(shape, dim):
    return lax.broadcasted_iota(jnp.int32, shape, dim)


def token_kernel(
    t1_ref, r1_ref, g1_ref, t2_ref, r2_ref, g2_ref, old_ref, new_ref, win_hbm, wout_hbm, o_ref,
    win, wout, tab, tabs, zbuf, pbuf, abuf, joined, rbuf, cbuf, sbuf, gbuf, own,
    wsem, tsend, trecv, zsend, zrecv, ysend, yrecv, rsend, rrecv, bsend, brecv,
):
    rows = t1_ref.shape[0]
    both = 2 * rows
    width = zbuf.shape[3]
    slab = pbuf.shape[2]
    cap = slab // 8
    inner = wout.shape[0]
    grp, ep = lax.axis_index("grp"), lax.axis_index("ep")
    x, low = grp % 4, grp // 4
    y, high, core = ep // 8, (ep // 2) % 4, ep % 2
    z = high * 2 + low
    sign = 1 - 2 * low
    me = y * 2 + core

    def at_z(step):
        there = (z + 8 + step) % 8
        return ((there % 2) * 4 + x, (y * 4 + there // 2) * 2 + core)

    def at_q(q):
        return (grp, ((q // 2) * 4 + high) * 2 + q % 2)

    z_to = (2 * sign, -3 * sign, -sign)
    z_from = (-2 * sign, -3 * sign, -sign)

    win_copy = pltpu.make_async_copy(win_hbm.at[0], win, wsem.at[0])
    wout_copy = pltpu.make_async_copy(wout_hbm.at[0], wout, wsem.at[1])
    win_copy.start()
    wout_copy.start()

    barrier = pltpu.get_barrier_semaphore()
    for step in (2, -2, -3 * sign, -sign):
        pl.semaphore_signal(barrier, inc=1, device_id=at_z(step), device_id_type=MESH)
    for off in range(1, 8):
        pl.semaphore_signal(barrier, inc=1, device_id=at_q((me + off) % 8), device_id_type=MESH)

    lane = iota((rows, 128), 1)

    def named_and_gates(r_ref, g_ref):
        named = jnp.zeros((rows, 128), F32)
        gate = jnp.zeros((rows, 128), F32)
        for k in range(TOP):
            hit = r_ref[:, k:k + 1] == lane
            named = named + jnp.where(hit, 1.0, 0.0)
            gate = gate + jnp.where(hit, g_ref[:, k:k + 1].astype(F32), 0.0)
        return named, gate

    same = (new_ref[...] == old_ref[...]).astype(F32).astype(BF)
    n1, gate1 = named_and_gates(r1_ref, g1_ref)
    n2, gate2 = named_and_gates(r2_ref, g2_ref)
    n2 = jnp.dot(n2[:, :32].astype(BF), same, preferred_element_type=F32)
    gate2 = jnp.dot(gate2[:, :32].astype(BF), same, preferred_element_type=F32)
    earlier = (iota((rows, rows), 1) < iota((rows, rows), 0)).astype(F32).astype(BF)

    def entries(named, gate, offset):
        rank = jnp.dot(earlier, named.astype(BF), preferred_element_type=F32)
        return jnp.where(named > 0.5, rank + offset, -1.0), pltpu.roll(gate, 32, 1)

    v1, w1 = entries(n1, gate1, 0.0)
    v2, w2 = entries(n2, gate2, float(cap))
    tab[:rows] = jnp.where(lane < 32, v1, w1).astype(BF)
    tab[rows:] = jnp.where(lane < 32, v2, w2).astype(BF)
    tabs[0] = tab[...]

    def place(k, carry):
        columns = pl.ds(pl.multiple_of(k * width, width), width)
        zbuf[k, 0, :rows] = t1_ref[:, columns]
        zbuf[k, 0, rows:] = t2_ref[:, columns]
        return carry

    lax.fori_loop(0, CHUNKS, place, 0)
    pl.semaphore_wait(barrier, 11)

    def tab_copy(m):
        return pltpu.make_async_remote_copy(
            src_ref=tab, dst_ref=tabs.at[m + 1], send_sem=tsend.at[m], recv_sem=trecv.at[m],
            device_id=at_z(z_to[m]), device_id_type=MESH)

    def z_copy(k, m):
        return pltpu.make_async_remote_copy(
            src_ref=zbuf.at[k, 0], dst_ref=zbuf.at[k, m + 1], send_sem=zsend.at[k, m], recv_sem=zrecv.at[k, m],
            device_id=at_z(z_to[m]), device_id_type=MESH)

    def y_copy(k, off):
        q = (me + off) % 8
        return pltpu.make_async_remote_copy(
            src_ref=pbuf.at[k, q], dst_ref=abuf.at[k, me], send_sem=ysend.at[k, off], recv_sem=yrecv.at[k, off],
            device_id=at_q(q), device_id_type=MESH)

    def r_copy(k, off):
        q = (me + 8 - off) % 8
        return pltpu.make_async_remote_copy(
            src_ref=rbuf.at[k, q], dst_ref=cbuf.at[k, me], send_sem=rsend.at[k, off], recv_sem=rrecv.at[k, off],
            device_id=at_q(q), device_id_type=MESH)

    def b_copy(k, m):
        return pltpu.make_async_remote_copy(
            src_ref=sbuf.at[k, m], dst_ref=gbuf.at[k, m], send_sem=bsend.at[k, m], recv_sem=brecv.at[k, m],
            device_id=at_z(z_from[m]), device_id_type=MESH)

    for m in range(3):
        tab_copy(m).start()

    def send_z(k, carry):
        for m in range(3):
            z_copy(k, m).start()
        return carry

    lax.fori_loop(0, CHUNKS, send_z, 0)
    for m in range(3):
        tab_copy(m).wait_recv()

    total = 8 * slab
    gathered = 4 * both
    table = tabs[...].reshape(gathered, 128)

    def expert_of(q):
        return (q // 2) * 8 + high * 2 + q % 2

    def slot_facts(shape, dim):
        n = iota(shape, dim)
        q = above(n, slab, 8)
        inside = n - q * slab
        j = above(inside, 2 * cap, 4)
        half = above(q, 2, 4)
        return half * 8 + high * 2 + (q - 2 * half), j, (inside - j * 2 * cap).astype(F32)

    e_row, _, _ = slot_facts((total, 128), 0)
    choose = (iota((total, 128), 1) == e_row).astype(F32).astype(BF)
    found = lax.dot_general(choose, table, (((1,), (1,)), ((), ())), preferred_element_type=F32)
    _, j_row, r_row = slot_facts((total, gathered), 0)
    pick = ((found == r_row) & (j_row == above(iota((total, gathered), 1), both, 4))).astype(F32).astype(BF)
    e_col, _, _ = slot_facts((128, total), 1)
    choose_v = (iota((128, total), 0) == e_col).astype(F32).astype(BF)
    choose_g = (iota((128, total), 0) == e_col + 32).astype(F32).astype(BF)
    found_v = jnp.dot(table, choose_v, preferred_element_type=F32)
    found_g = jnp.dot(table, choose_g, preferred_element_type=F32)
    _, j_col, r_col = slot_facts((gathered, total), 1)
    mix = jnp.where(
        (found_v == r_col) & (j_col == above(iota((gathered, total), 0), both, 4)), found_g, 0.0).astype(BF)

    def pack(k, carry):
        for m in range(3):
            z_copy(k, m).wait_recv()
        packed = jnp.dot(pick, zbuf[k].reshape(gathered, width), preferred_element_type=F32)
        pbuf[k] = packed.reshape(8, slab, width).astype(BF)
        for off in range(1, 8):
            y_copy(k, off).start()
        abuf[k, me] = pbuf[k, me]
        return carry

    lax.fori_loop(0, CHUNKS, pack, 0)
    win_copy.wait()
    joined[...] = jnp.zeros_like(joined)

    def project(k, carry):
        for off in range(1, 8):
            y_copy(k, off).wait_recv()
        block = abuf[k].reshape(total, width)
        joined[...] += jnp.dot(
            block, win[pl.ds(pl.multiple_of(k * width, width), width), :], preferred_element_type=F32)
        return carry

    lax.fori_loop(0, CHUNKS, project, 0)
    gate_part = joined[:, :inner]
    hidden = (gate_part / (1.0 + jnp.exp(-gate_part)) * joined[:, inner:]).astype(BF)
    wout_copy.wait()

    def expand(k, carry):
        result = jnp.dot(
            hidden, wout[:, pl.ds(pl.multiple_of(k * width, width), width)], preferred_element_type=F32)
        rbuf[k] = result.reshape(8, slab, width).astype(BF)
        for off in range(1, 8):
            r_copy(k, off).start()
        cbuf[k, me] = rbuf[k, me]
        return carry

    lax.fori_loop(0, CHUNKS, expand, 0)

    def combine(k, carry):
        for off in range(1, 8):
            r_copy(k, off).wait_recv()
        part = jnp.dot(mix, cbuf[k].reshape(total, width), preferred_element_type=F32)
        own[k] = part[:both]
        sbuf[k] = part[both:].reshape(3, both, width).astype(BF)
        for m in range(3):
            b_copy(k, m).start()
        return carry

    lax.fori_loop(0, CHUNKS, combine, 0)

    def finish(k, carry):
        for m in range(3):
            b_copy(k, m).wait_recv()
        sums = own[k]
        for m in range(3):
            sums = sums + gbuf[k, m].astype(F32)
        o_ref[:, pl.ds(pl.multiple_of(k * width, width), width)] = sums
        return carry

    lax.fori_loop(0, CHUNKS, finish, 0)
    for m in range(3):
        tab_copy(m).wait_send()

    def drain(k, carry):
        for m in range(3):
            z_copy(k, m).wait_send()
            b_copy(k, m).wait_send()
        for off in range(1, 8):
            y_copy(k, off).wait_send()
            r_copy(k, off).wait_send()
        return carry

    lax.fori_loop(0, CHUNKS, drain, 0)


def routed(t1, r1, g1, t2, r2, g2, old_table, new_table, gate_up, down_proj):
    rows, features = t1.shape
    both = 2 * rows
    inner = down_proj.shape[1]
    experts = old_table.shape[0]
    cap = 3 * rows * TOP // (2 * experts)
    slab = 8 * cap
    width = features // CHUNKS
    old_row = jnp.pad(old_table, (0, 128 - experts), constant_values=-1)[None, :]
    vmem = pl.BlockSpec(memory_space=pltpu.VMEM)
    hbm = pl.BlockSpec(memory_space=pl.ANY)
    dma = pltpu.SemaphoreType.DMA
    return pl.pallas_call(
        token_kernel,
        out_shape=jax.ShapeDtypeStruct((both, features), F32),
        in_specs=[vmem] * 8 + [hbm] * 2,
        out_specs=vmem,
        scratch_shapes=[
            pltpu.VMEM((features, 2 * inner), BF),
            pltpu.VMEM((inner, features), BF),
            pltpu.VMEM((both, 128), BF),
            pltpu.VMEM((4, both, 128), BF),
            pltpu.VMEM((CHUNKS, 4, both, width), BF),
            pltpu.VMEM((CHUNKS, 8, slab, width), BF),
            pltpu.VMEM((CHUNKS, 8, slab, width), BF),
            pltpu.VMEM((8 * slab, 2 * inner), F32),
            pltpu.VMEM((CHUNKS, 8, slab, width), BF),
            pltpu.VMEM((CHUNKS, 8, slab, width), BF),
            pltpu.VMEM((CHUNKS, 3, both, width), BF),
            pltpu.VMEM((CHUNKS, 3, both, width), BF),
            pltpu.VMEM((CHUNKS, both, width), F32),
            dma((2,)), dma((3,)), dma((3,)),
            dma((CHUNKS, 3)), dma((CHUNKS, 3)),
            dma((CHUNKS, 8)), dma((CHUNKS, 8)),
            dma((CHUNKS, 8)), dma((CHUNKS, 8)),
            dma((CHUNKS, 3)), dma((CHUNKS, 3)),
        ],
        compiler_params=pltpu.CompilerParams(
            collective_id=0, has_side_effects=True, vmem_limit_bytes=50 << 20),
        cost_estimate=pl.CostEstimate(flops=8_000_000_000, bytes_accessed=200_000_000, transcendentals=0),
        name="routed_tokens",
    )(t1, r1, g1, t2, r2, g2, old_row, new_table[:, None], gate_up, down_proj)


def local(
    tokens_one,
    routes_one,
    gates_one,
    tokens_two,
    routes_two,
    gates_two,
    old_table,
    new_table,
    gate_up,
    down_proj,
    norm_gain,
    kv_weight,
):
    weight_in = gate_up[0]
    weight_out = down_proj[0]
    ep_size = lax.axis_size("ep")
    grp_size = lax.axis_size("grp")
    numbers = jnp.arange(ep_size, dtype=jnp.int32)
    sources_new = jnp.sum((new_table[:, None] == old_table[None, :]).astype(jnp.int32) * numbers[None, :], axis=1)
    features, inner = weight_in.shape[0], weight_out.shape[0]
    part = features // grp_size
    start = lax.axis_index("grp") * part
    piece_in = lax.dynamic_slice_in_dim(weight_in, start, part, 0)
    piece_out = lax.dynamic_slice_in_dim(weight_out, start, part, 1)
    n_in, n_out = piece_in.size // ep_size, piece_out.size // ep_size
    pieces = jnp.concatenate(
        [piece_in.reshape(ep_size, n_in // 128, 128), piece_out.reshape(ep_size, n_out // 128, 128)], axis=1
    )
    spread = lax.all_to_all(pieces, "ep", split_axis=0, concat_axis=0, tiled=True)
    collected = lax.all_to_all(spread[sources_new], "ep", split_axis=0, concat_axis=0, tiled=True)
    cut = n_in // 128
    gate_up_new = collected[:, :cut].reshape(1, part, 2 * inner)
    down_proj_new = collected[:, cut:].reshape(1, inner, part)

    rows = tokens_one.shape[0]
    mixture = routed(
        tokens_one, routes_one, gates_one, tokens_two, routes_two, gates_two, old_table, new_table,
        gate_up, down_proj)
    tokens = jnp.concatenate([tokens_one, tokens_two], axis=0)
    out = (tokens.astype(F32) + mixture).astype(BF)
    values = out.astype(F32)
    inverse_rms = lax.rsqrt(jnp.mean(values * values, axis=-1, keepdims=True) + 1e-06)
    normed = (values * inverse_rms * norm_gain.astype(F32)).astype(BF)
    projected = jnp.dot(
        normed,
        lax.all_gather(kv_weight, "grp", axis=1, tiled=True),
        preferred_element_type=F32,
    ).astype(BF)
    return (out[:rows], projected[:rows], out[rows:], projected[rows:], gate_up_new, down_proj_new)


def solution(mesh):
    split = P(("grp", "ep"), None)
    return jax.shard_map(
        local,
        mesh=mesh,
        in_specs=(split,) * 6 + (P(), P(), P("ep", None, None), P("ep", None, None), P(), P(None, "grp")),
        out_specs=(split,) * 4 + (P("ep", "grp", None), P("ep", None, "grp")),
        check_vma=False,
    )
```

time: 301 us -> 206 us (0.68)
  waiting for transfers between devices: 199 us -> 39.8 us
  Pallas kernels: 0 us -> 112 us
  local copies, waits for them, and re-layouts: 34.5 us -> 12.9 us
  matrix products: 19.8 us -> 3.08 us
  starting transfers between devices: 29.5 us -> 19.9 us
    all_to_all x2 -> x0, waiting for transfers between devices: 163 us -> none  [the longest x1 91.4 us: local(): lax.all_to_all(result.reshape(ep_size, 2 * capacity, features), 'ep', spl...]
    pallas_call x0 -> x1, Pallas kernels: none -> 112 us  [routed(): pl.pallas_call(token_kernel, out_shape=jax.ShapeDtypeStruct((both, featur...]
    all_to_all x1, waiting for transfers between devices: 18.4 us -> 39.1 us  [local(): lax.all_to_all(pieces, 'ep', split_axis=0, concat_axis=0, tiled=True)]
    dot_general x6 -> x0, matrix products: 16.8 us -> none  [the longest x1 6.89 us: local(): joined = jnp.dot(activation, weight_in, preferred_element_type=jnp.float32)]
    all_to_all x1, waiting for transfers between devices: 16.5 us -> 0.01 us  [local(): lax.all_to_all(spread[sources_new], 'ep', split_axis=0, concat_axis=0, ti...]
    reshape x3 -> x0, local copies, waits for them, and re-layouts: 13 us -> none  [the longest x1 4.34 us: local(): activation = arrived.reshape(ep_size * 2 * capacity, features)]
    all_to_all x2 -> x0, starting transfers between devices: 11.9 us -> none  [the longest x1 7.28 us: local(): lax.all_to_all(packed.reshape(ep_size, 2 * capacity, features), 'ep', spl...]
  transfers between devices with their start and end apart: 5 -> 3, of which waited for: 4 -> 1; matrix products, arithmetic and copies ran while one was open for 15% -> 7% of each run, Pallas kernels for 0% -> 55%
where the time goes in v2:
time: 206 us; the launch traced here: 203 us
  Pallas kernels  112 us (54%)
  waiting for transfers between devices  39.8 us (19%)
  starting transfers between devices  19.9 us (10%)
  between operations  14.2 us (7%)
  local copies, waits for them, and re-layouts  12.9 us (6%)
  matrix products  3.08 us (1%)
    pallas_call x1, Pallas kernels, routed(): pl.pallas_call(token_kernel, out_shape=jax.ShapeDtypeStruct((both, featur...  112 us
    all_to_all x1, waiting for transfers between devices, local(): lax.all_to_all(pieces, 'ep', split_axis=0, concat_axis=0, tiled=True)  39.1 us
    all_to_all x1, starting transfers between devices, local(): lax.all_to_all(pieces, 'ep', split_axis=0, concat_axis=0, tiled=True)  12.8 us
    all_to_all x1, starting transfers between devices, local(): lax.all_to_all(spread[sources_new], 'ep', split_axis=0, concat_axis=0, ti...  7.07 us
  transfers between devices with their start and end apart: 3, of which 1 were waited for; matrix products, arithmetic and copies ran while one was open for 7% of the time, Pallas kernels for 55%

profile of v2, /device:TPU:1, one launch (start us, length us, event | category | flops | bytes accessed | tf_op | source)
XLA Modules:
  0.0 203.0 jit_solution(3408806803108059406)
XLA Ops:
  7.2 0.0 all-gather.2.cloned.1.call-start
  7.2 0.7 all-gather.2.cloned.1.call-update
  7.9 1.0 constant_dynamic-slice_fusion
  8.9 0.2 reshape.53
  9.1 1.2 constant_dynamic-slice_fusion.1
  10.3 0.9 reshape.52
  11.1 0.0 copy-start.8
  11.1 0.0 copy-start.9
  11.1 1.1 pad_maximum_fusion
  12.3 12.8 %all-to-all-start = ((bf16[32,132,128]{2,1,0:T(8,128)(2,1)}), bf16[32,132,128]{2,1,0:T(8,128)(2,1)}, u32[]{:S(2)}, u32[]{:S(2)}) async-start(bf16[32,132,128]{2,1,0:T(8,128)(2,1)} %pad_maximum_fusion), calls=%async_computation | async-start | bytes 2228224 | tf_op jit(solution)/shard_map/all_to_all | solution.py:317
  25.1 0.2 select_reduce_fusion
  25.3 0.0 copy-start.6
  25.3 0.0 copy-start.4
  25.4 0.0 copy-start
  25.4 0.0 copy-start.1
  25.4 39.1 %all-to-all-done = bf16[32,132,128]{2,1,0:T(8,128)(2,1)} async-done(((bf16[32,132,128]{2,1,0:T(8,128)(2,1)}), bf16[32,132,128]{2,1,0:T(8,128)(2,1)}, u32[]{:S(2)}, u32[]{:S(2)}) %all-to-all-start) | async-done | bytes 1081376 | tf_op jit(solution)/shard_map/all_to_all | solution.py:317
  64.5 3.0 %gather_fusion = bf16[32,132,128]{2,1,0:T(8,128)(2,1)} fusion(bf16[32,132,128]{2,1,0:T(8,128)(2,1)} %all-to-all-done, s32[1024]{0:T(1024)S(1)} %pad_clamp_fusion), kind=kCustom, calls=%fused_computation | custom fusion | bytes 2162816 | tf_op jit(solution)/shard_map/gather | solution.py:318
  67.5 7.1 %all-to-all-start.1 = ((bf16[32,132,128]{2,1,0:T(8,128)(2,1)}), bf16[32,132,128]{2,1,0:T(8,128)(2,1)}, u32[]{:S(2)}, u32[]{:S(2)}) async-start(bf16[32,132,128]{2,1,0:T(8,128)(2,1)} %gather_fusion), calls=%async_computation.1 | async-start | bytes 2228224 | tf_op jit(solution)/shard_map/all_to_all | solution.py:318
  74.6 0.1 copy.28.r1_ref
  74.7 0.1 copy.29.g1_ref
  74.8 0.1 copy.30.r2_ref
  74.9 0.1 copy.31.g2_ref
  75.0 0.1 copy.32.new_ref
  75.1 111.6 %routed_tokens.1 = f32[64,2048]{1,0:T(8,128)S(1)} custom-call(bf16[32,2048]{1,0:T(8,128)(2,1)S(1)} %copy-done, s32[32,6]{1,0:T(8,128)S(1)} %copy.28.r1_ref, bf16[32,6]{1,0:T(8,128)(2,1)S(1)} %copy.29.g1_ref, bf16[32,2048]{1,0:T(8,128)(2,1)S(1)} %copy-done.1, s32[32,6]{1,0:T(8,128)S(1)} %copy.30.r2_ref, bf16[32,6]{1,0:T(8,128)(2,1)S(1)} %copy.31.g2_ref, ...), custom_call_target="tpu_custom_call" | custom-call | flops 8000000000 | bytes 200000000 | tf_op jit(solution)/shard_map/routed_tokens/pallas_call | solution.py:256
  186.7 0.2 fusion
  186.9 0.7 fusion.7
  187.6 1.2 slice.30
  188.8 1.7 reshape.54
  190.5 1.0 slice.31
  191.5 0.9 reshape.55
  192.4 3.1 %convolution_convert_fusion = bf16[64,1024]{1,0:T(8,128)(2,1)S(1)} fusion(bf16[2048,1024]{1,0:T(8,128)(2,1)} %all-gather.2.cloned.1.call-done, bf16[64,2048]{1,0:T(8,128)(2,1)S(1)} %get-tuple-element.7, f32[2048]{0:T(1024)S(1)} %convert_element_type.22, f32[64]{0:T(128)S(1)} %add_rsqrt_fusion), kind=kOutput, calls=%fused_computation.1 | convolution fusion | flops 269025280 | bytes 4595968 | tf_op jit(solution)/shard_map/dot_general | solution.py:332
  195.5 0.7 fusion.8
  (21 shorter events, 0.1 us)
Async XLA Ops:
  7.2 185.3 %all-gather.2.cloned.1.call-start = ((), (), s32[]{:S(2)}) async-start(), calls=%async_computation.2 | async-start | bytes 4718592 | tf_op jit(solution)/shard_map/all_gather | solution.py:334
  11.1 14.0 %copy-start.8 = (s32[32]{0:T(128)S(1)}, s32[32]{0:T(128)}, u32[]{:S(2)}) copy-start(s32[32]{0:T(128)} %param.19) | copy-start | bytes 388
  11.1 14.0 %copy-start.9 = (s32[32]{0:T(128)S(1)}, s32[32]{0:T(128)}, u32[]{:S(2)}) copy-start(s32[32]{0:T(128)} %param.18) | copy-start | bytes 388
  12.3 52.2 %all-to-all-start = ((bf16[32,132,128]{2,1,0:T(8,128)(2,1)}), bf16[32,132,128]{2,1,0:T(8,128)(2,1)}, u32[]{:S(2)}, u32[]{:S(2)}) async-start(bf16[32,132,128]{2,1,0:T(8,128)(2,1)} %pad_maximum_fusion), calls=%async_computation | async-start | bytes 2228224 | tf_op jit(solution)/shard_map/all_to_all | solution.py:317
  25.3 49.3 %copy-start.3 = (s32[32,6]{0,1:T(8,128)S(1)}, s32[32,6]{0,1:T(8,128)}, u32[]{:S(2)}) copy-start(s32[32,6]{0,1:T(8,128)} %param.13) | copy-start | bytes 2308
  25.3 49.3 %copy-start.6 = (bf16[32,6]{0,1:T(8,128)(2,1)S(1)}, bf16[32,6]{0,1:T(8,128)(2,1)}, u32[]{:S(2)}) copy-start(bf16[32,6]{0,1:T(8,128)(2,1)} %param.14) | copy-start | bytes 1156
  25.3 49.4 %copy-start.4 = (s32[32,6]{0,1:T(8,128)S(1)}, s32[32,6]{0,1:T(8,128)}, u32[]{:S(2)}) copy-start(s32[32,6]{0,1:T(8,128)} %param.16) | copy-start | bytes 2308
  25.3 49.5 %copy-start.7 = (bf16[32,6]{0,1:T(8,128)(2,1)S(1)}, bf16[32,6]{0,1:T(8,128)(2,1)}, u32[]{:S(2)}) copy-start(bf16[32,6]{0,1:T(8,128)(2,1)} %param.17) | copy-start | bytes 1156
  25.4 49.7 %copy-start.5 = (bf16[2048]{0:T(1024)(128)(2,1)S(1)}, bf16[2048]{0:T(1024)(128)(2,1)}, u32[]{:S(2)}) copy-start(bf16[2048]{0:T(1024)(128)(2,1)} %param.22) | copy-start | bytes 12292
  25.4 49.7 %copy-start = (bf16[32,2048]{1,0:T(8,128)(2,1)S(1)}, bf16[32,2048]{1,0:T(8,128)(2,1)}, u32[]{:S(2)}) copy-start(bf16[32,2048]{1,0:T(8,128)(2,1)} %t1_ref.1) | copy-start | bytes 393220
  25.4 49.7 %copy-start.1 = (bf16[32,2048]{1,0:T(8,128)(2,1)S(1)}, bf16[32,2048]{1,0:T(8,128)(2,1)}, u32[]{:S(2)}) copy-start(bf16[32,2048]{1,0:T(8,128)(2,1)} %t2_ref.1) | copy-start | bytes 393220
  25.4 49.7 %copy-start.2 = (bf16[1,704,2048]{2,1,0:T(8,128)(2,1)S(1)}, bf16[1,704,2048]{2,1,0:T(8,128)(2,1)}, u32[]{:S(2)}) copy-start(bf16[1,704,2048]{2,1,0:T(8,128)(2,1)} %wout_hbm.1) | copy-start | bytes 8650756
  67.5 120.2 %all-to-all-start.1 = ((bf16[32,132,128]{2,1,0:T(8,128)(2,1)}), bf16[32,132,128]{2,1,0:T(8,128)(2,1)}, u32[]{:S(2)}, u32[]{:S(2)}) async-start(bf16[32,132,128]{2,1,0:T(8,128)(2,1)} %gather_fusion), calls=%async_computation.1 | async-start | bytes 2228224 | tf_op jit(solution)/shard_map/all_to_all | solution.py:318
Sparse Core Ops, SparseCore 0:
  9.7 118.5 all-gather.1

commit v3 on v2

--- a/solution.py
+++ b/solution.py
@@ -23,9 +23,12 @@
 
 
 def token_kernel(
-    t1_ref, r1_ref, g1_ref, t2_ref, r2_ref, g2_ref, old_ref, new_ref, win_hbm, wout_hbm, o_ref,
-    win, wout, tab, tabs, zbuf, pbuf, abuf, joined, rbuf, cbuf, sbuf, gbuf, own,
-    wsem, tsend, trecv, zsend, zrecv, ysend, yrecv, rsend, rrecv, bsend, brecv,
+    t1_ref, r1_ref, g1_ref, t2_ref, r2_ref, g2_ref, old_ref, new_ref, win_hbm, wout_hbm,
+    o_ref, in_new, out_new,
+    r1v, g1v, r2v, g2v, oldv, newv, srcv, srcs, mid_in, mid_out, pick_in, pick_out, fin_out,
+    win, wout, ttab, tab, tabs, zbuf, pbuf, abuf, joined, rbuf, cbuf, sbuf, gbuf, own,
+    wsem, lsem, tsend, trecv, zsend, zrecv, ysend, yrecv, rsend, rrecv, bsend, brecv,
+    hsend, hrecv, fsend, frecv, selfsem,
 ):
     rows = t1_ref.shape[0]
     both = 2 * rows
@@ -50,53 +53,143 @@
     z_to = (2 * sign, -3 * sign, -sign)
     z_from = (-2 * sign, -3 * sign, -sign)
 
+    copies = [
+        pltpu.make_async_copy(r1_ref, r1v, lsem.at[0]),
+        pltpu.make_async_copy(g1_ref, g1v, lsem.at[1]),
+        pltpu.make_async_copy(r2_ref, r2v, lsem.at[2]),
+        pltpu.make_async_copy(g2_ref, g2v, lsem.at[3]),
+        pltpu.make_async_copy(old_ref, oldv, lsem.at[7]),
+        pltpu.make_async_copy(new_ref, newv, lsem.at[8]),
+    ]
+    for copy in copies:
+        copy.start()
+
+    def place_copy(k, b):
+        t_ref = t1_ref if b == 0 else t2_ref
+        return pltpu.make_async_copy(
+            t_ref.at[:, pl.ds(pl.multiple_of(k * width, width), width)], zbuf.at[k, 0, pl.ds(b * rows, rows)],
+            lsem.at[4 + b])
+
+    for k in range(CHUNKS):
+        for b in range(2):
+            place_copy(k, b).start()
     win_copy = pltpu.make_async_copy(win_hbm.at[0], win, wsem.at[0])
     wout_copy = pltpu.make_async_copy(wout_hbm.at[0], wout, wsem.at[1])
     win_copy.start()
     wout_copy.start()
 
+    def at_ep(e):
+        return (grp, e)
+
     barrier = pltpu.get_barrier_semaphore()
     for step in (2, -2, -3 * sign, -sign):
         pl.semaphore_signal(barrier, inc=1, device_id=at_z(step), device_id_type=MESH)
-    for off in range(1, 8):
-        pl.semaphore_signal(barrier, inc=1, device_id=at_q((me + off) % 8), device_id_type=MESH)
-
-    lane = iota((rows, 128), 1)
+
+    def greet(off, carry):
+        pl.semaphore_signal(barrier, inc=1, device_id=at_ep((ep + off) % 32), device_id_type=MESH)
+        return carry
+
+    lax.fori_loop(1, 32, greet, 0)
+
+    for copy in copies:
+        copy.wait()
+    square = (32, 32)
 
     def named_and_gates(r_ref, g_ref):
-        named = jnp.zeros((rows, 128), F32)
-        gate = jnp.zeros((rows, 128), F32)
+        named = jnp.zeros((32, rows), F32)
+        gate = jnp.zeros((32, rows), F32)
+        number = iota((32, rows), 0)
         for k in range(TOP):
-            hit = r_ref[:, k:k + 1] == lane
+            hit = r_ref[k:k + 1, :] == number
             named = named + jnp.where(hit, 1.0, 0.0)
-            gate = gate + jnp.where(hit, g_ref[:, k:k + 1].astype(F32), 0.0)
+            gate = gate + jnp.where(hit, g_ref[k:k + 1, :].astype(F32), 0.0)
         return named, gate
 
-    same = (new_ref[...] == old_ref[...]).astype(F32).astype(BF)
-    n1, gate1 = named_and_gates(r1_ref, g1_ref)
-    n2, gate2 = named_and_gates(r2_ref, g2_ref)
-    n2 = jnp.dot(n2[:, :32].astype(BF), same, preferred_element_type=F32)
-    gate2 = jnp.dot(gate2[:, :32].astype(BF), same, preferred_element_type=F32)
-    earlier = (iota((rows, rows), 1) < iota((rows, rows), 0)).astype(F32).astype(BF)
-
-    def entries(named, gate, offset):
-        rank = jnp.dot(earlier, named.astype(BF), preferred_element_type=F32)
-        return jnp.where(named > 0.5, rank + offset, -1.0), pltpu.roll(gate, 32, 1)
-
-    v1, w1 = entries(n1, gate1, 0.0)
-    v2, w2 = entries(n2, gate2, float(cap))
-    tab[:rows] = jnp.where(lane < 32, v1, w1).astype(BF)
-    tab[rows:] = jnp.where(lane < 32, v2, w2).astype(BF)
+    diagonal = iota(square, 0) == iota(square, 1)
+    old_column = jnp.sum(jnp.where(diagonal, oldv[...].astype(F32), 0.0), axis=1, keepdims=True)
+    same = (old_column == newv[...].astype(F32)).astype(F32)
+    found_at = jnp.sum(same * iota(square, 0).astype(F32), axis=0, keepdims=True)
+    srcv[:, :32] = found_at.astype(jnp.int32)
+    src_copy = pltpu.make_async_copy(srcv, srcs, lsem.at[6])
+    src_copy.start()
+    same = same.astype(BF)
+    n1, gate1 = named_and_gates(r1v, g1v)
+    n2, gate2 = named_and_gates(r2v, g2v)
+    n2 = jnp.dot(same, n2.astype(BF), preferred_element_type=F32)
+    gate2 = jnp.dot(same, gate2.astype(BF), preferred_element_type=F32)
+    earlier = (iota((rows, rows), 0) < iota((rows, rows), 1)).astype(F32).astype(BF)
+
+    def entries(named, offset):
+        rank = jnp.dot(named.astype(BF), earlier, preferred_element_type=F32)
+        return jnp.where(named > 0.5, rank + offset, -1.0)
+
+    ttab[...] = jnp.zeros_like(ttab)
+    ttab[:32, :rows] = entries(n1, 0.0)
+    ttab[:32, rows:both] = entries(n2, float(cap))
+    ttab[32:64, :rows] = gate1
+    ttab[32:64, rows:both] = gate2
+    tab[...] = jnp.transpose(ttab[...])[:both].astype(BF)
     tabs[0] = tab[...]
-
-    def place(k, carry):
-        columns = pl.ds(pl.multiple_of(k * width, width), width)
-        zbuf[k, 0, :rows] = t1_ref[:, columns]
-        zbuf[k, 0, rows:] = t2_ref[:, columns]
-        return carry
-
-    lax.fori_loop(0, CHUNKS, place, 0)
-    pl.semaphore_wait(barrier, 11)
+    for b in range(2):
+        for k in range(CHUNKS):
+            place_copy(k, b).wait()
+    pl.semaphore_wait(barrier, 35)
+
+    def part_in(j):
+        return win_hbm.at[0, pl.ds(pl.multiple_of(grp * 256 + j * 8, 8), 8), :]
+
+    def part_out(j):
+        p = j // 2
+        return wout_hbm.at[
+            0, pl.ds(pl.multiple_of(8 * ((11 * p) // 2), 8), 48),
+            pl.ds(pl.multiple_of(grp * 256 + (j % 2) * 128, 128), 128)]
+
+    def ep_of(dy, dz, dc):
+        return (((y + dy) % 4) * 4 + (high + dz) % 4) * 2 + (core + dc) % 2
+
+    def ep_at(n, back):
+        dy, dz, dc = (n // 2) % 4, n // 8, n % 2
+        if back:
+            return ep_of(4 - dy, 4 - dz, dc)
+        return ep_of(dy, dz, dc)
+
+    def spread_copies(n):
+        j = ep_at(n, False)
+        return [
+            pltpu.make_async_remote_copy(
+                src_ref=part_in(j), dst_ref=mid_in.at[ep], send_sem=hsend.at[0, n], recv_sem=hrecv.at[0, n],
+                device_id=at_ep(j), device_id_type=MESH),
+            pltpu.make_async_remote_copy(
+                src_ref=part_out(j), dst_ref=mid_out.at[ep], send_sem=hsend.at[1, n], recv_sem=hrecv.at[1, n],
+                device_id=at_ep(j), device_id_type=MESH)]
+
+    def fetch_copies(n):
+        s = ep_at(n, False)
+        return [
+            pltpu.make_async_remote_copy(
+                src_ref=pick_in.at[s], dst_ref=in_new.at[pl.ds(pl.multiple_of(ep * 8, 8), 8), :],
+                send_sem=fsend.at[0, n], recv_sem=frecv.at[0, n],
+                device_id=at_ep(s), device_id_type=MESH),
+            pltpu.make_async_remote_copy(
+                src_ref=pick_out.at[s], dst_ref=fin_out.at[ep], send_sem=fsend.at[1, n], recv_sem=frecv.at[1, n],
+                device_id=at_ep(s), device_id_type=MESH)]
+
+    def start_spread(n, carry):
+        for copy in spread_copies(n):
+            copy.start()
+        return carry
+
+    def wait_spread(n, carry):
+        for copy in spread_copies(n):
+            copy.wait_recv()
+        return carry
+
+    own_spread = [
+        pltpu.make_async_copy(part_in(ep), mid_in.at[ep], selfsem.at[0]),
+        pltpu.make_async_copy(part_out(ep), mid_out.at[ep], selfsem.at[1])]
+    own_fetch = [
+        pltpu.make_async_copy(pick_in.at[ep], in_new.at[pl.ds(pl.multiple_of(ep * 8, 8), 8), :], selfsem.at[2]),
+        pltpu.make_async_copy(pick_out.at[ep], fin_out.at[ep], selfsem.at[3])]
 
     def tab_copy(m):
         return pltpu.make_async_remote_copy(
@@ -134,6 +227,9 @@
         return carry
 
     lax.fori_loop(0, CHUNKS, send_z, 0)
+    for copy in own_spread:
+        copy.start()
+    lax.fori_loop(1, 8, start_spread, 0)
     for m in range(3):
         tab_copy(m).wait_recv()
 
@@ -177,6 +273,7 @@
         return carry
 
     lax.fori_loop(0, CHUNKS, pack, 0)
+    lax.fori_loop(8, 32, start_spread, 0)
     win_copy.wait()
     joined[...] = jnp.zeros_like(joined)
 
@@ -204,6 +301,28 @@
 
     lax.fori_loop(0, CHUNKS, expand, 0)
 
+    src_copy.wait()
+    for copy in own_spread:
+        copy.wait()
+    lax.fori_loop(1, 32, wait_spread, 0)
+
+    def choose_parts(s, carry):
+        wanted = jnp.minimum(jnp.maximum(srcs[0, s], 0), 31)
+        pick_in[s] = mid_in[wanted]
+        pick_out[s] = mid_out[wanted]
+        return carry
+
+    lax.fori_loop(0, 32, choose_parts, 0)
+
+    def start_fetch(n, carry):
+        for copy in fetch_copies(n):
+            copy.start()
+        return carry
+
+    lax.fori_loop(1, 32, start_fetch, 0)
+    for copy in own_fetch:
+        copy.start()
+
     def combine(k, carry):
         for off in range(1, 8):
             r_copy(k, off).wait_recv()
@@ -226,6 +345,22 @@
         return carry
 
     lax.fori_loop(0, CHUNKS, finish, 0)
+
+    def end_fetch(n, carry):
+        for copy in spread_copies(n):
+            copy.wait_send()
+        for copy in fetch_copies(n):
+            copy.wait_send()
+            copy.wait_recv()
+        return carry
+
+    for copy in own_fetch:
+        copy.wait()
+    lax.fori_loop(1, 32, end_fetch, 0)
+    for p in range(16):
+        first, count = 8 * ((11 * p) // 2), 40 + 8 * (p % 2)
+        for h in range(2):
+            out_new[first:first + count, 128 * h:128 * h + 128] = fin_out[2 * p + h, :count]
     for m in range(3):
         tab_copy(m).wait_send()
 
@@ -249,18 +384,36 @@
     cap = 3 * rows * TOP // (2 * experts)
     slab = 8 * cap
     width = features // CHUNKS
-    old_row = jnp.pad(old_table, (0, 128 - experts), constant_values=-1)[None, :]
     vmem = pl.BlockSpec(memory_space=pltpu.VMEM)
-    hbm = pl.BlockSpec(memory_space=pl.ANY)
+    hbm = pl.BlockSpec(memory_space=pltpu.HBM)
     dma = pltpu.SemaphoreType.DMA
+    part = features // 8
     return pl.pallas_call(
         token_kernel,
-        out_shape=jax.ShapeDtypeStruct((both, features), F32),
-        in_specs=[vmem] * 8 + [hbm] * 2,
-        out_specs=vmem,
+        out_shape=(
+            jax.ShapeDtypeStruct((both, features), F32),
+            jax.ShapeDtypeStruct((part, 2 * inner), BF),
+            jax.ShapeDtypeStruct((inner, part), BF),
+        ),
+        in_specs=[hbm] * 10,
+        out_specs=(vmem, hbm, vmem),
         scratch_shapes=[
+            pltpu.VMEM((TOP, rows), jnp.int32),
+            pltpu.VMEM((TOP, rows), BF),
+            pltpu.VMEM((TOP, rows), jnp.int32),
+            pltpu.VMEM((TOP, rows), BF),
+            pltpu.VMEM((1, 32), jnp.int32),
+            pltpu.VMEM((1, 32), jnp.int32),
+            pltpu.VMEM((1, 128), jnp.int32),
+            pltpu.SMEM((1, 128), jnp.int32),
+            pltpu.VMEM((32, 8, 2 * inner), BF),
+            pltpu.VMEM((32, 48, 128), BF),
+            pltpu.VMEM((32, 8, 2 * inner), BF),
+            pltpu.VMEM((32, 48, 128), BF),
+            pltpu.VMEM((32, 48, 128), BF),
             pltpu.VMEM((features, 2 * inner), BF),
             pltpu.VMEM((inner, features), BF),
+            pltpu.VMEM((128, 128), F32),
             pltpu.VMEM((both, 128), BF),
             pltpu.VMEM((4, both, 128), BF),
             pltpu.VMEM((CHUNKS, 4, both, width), BF),
@@ -272,17 +425,18 @@
             pltpu.VMEM((CHUNKS, 3, both, width), BF),
             pltpu.VMEM((CHUNKS, 3, both, width), BF),
             pltpu.VMEM((CHUNKS, both, width), F32),
-            dma((2,)), dma((3,)), dma((3,)),
+            dma((2,)), dma((9,)), dma((3,)), dma((3,)),
             dma((CHUNKS, 3)), dma((CHUNKS, 3)),
             dma((CHUNKS, 8)), dma((CHUNKS, 8)),
             dma((CHUNKS, 8)), dma((CHUNKS, 8)),
             dma((CHUNKS, 3)), dma((CHUNKS, 3)),
+            dma((2, 32)), dma((2, 32)), dma((2, 32)), dma((2, 32)), dma((4,)),
         ],
         compiler_params=pltpu.CompilerParams(
-            collective_id=0, has_side_effects=True, vmem_limit_bytes=50 << 20),
+            collective_id=0, has_side_effects=True, vmem_limit_bytes=60 << 20),
         cost_estimate=pl.CostEstimate(flops=8_000_000_000, bytes_accessed=200_000_000, transcendentals=0),
         name="routed_tokens",
-    )(t1, r1, g1, t2, r2, g2, old_row, new_table[:, None], gate_up, down_proj)
+    )(t1, r1.T, g1.T, t2, r2.T, g2.T, old_table[None, :], new_table[None, :], gate_up, down_proj)
 
 
 def local(
@@ -299,29 +453,8 @@
     norm_gain,
     kv_weight,
 ):
-    weight_in = gate_up[0]
-    weight_out = down_proj[0]
-    ep_size = lax.axis_size("ep")
-    grp_size = lax.axis_size("grp")
-    numbers = jnp.arange(ep_size, dtype=jnp.int32)
-    sources_new = jnp.sum((new_table[:, None] == old_table[None, :]).astype(jnp.int32) * numbers[None, :], axis=1)
-    features, inner = weight_in.shape[0], weight_out.shape[0]
-    part = features // grp_size
-    start = lax.axis_index("grp") * part
-    piece_in = lax.dynamic_slice_in_dim(weight_in, start, part, 0)
-    piece_out = lax.dynamic_slice_in_dim(weight_out, start, part, 1)
-    n_in, n_out = piece_in.size // ep_size, piece_out.size // ep_size
-    pieces = jnp.concatenate(
-        [piece_in.reshape(ep_size, n_in // 128, 128), piece_out.reshape(ep_size, n_out // 128, 128)], axis=1
-    )
-    spread = lax.all_to_all(pieces, "ep", split_axis=0, concat_axis=0, tiled=True)
-    collected = lax.all_to_all(spread[sources_new], "ep", split_axis=0, concat_axis=0, tiled=True)
-    cut = n_in // 128
-    gate_up_new = collected[:, :cut].reshape(1, part, 2 * inner)
-    down_proj_new = collected[:, cut:].reshape(1, inner, part)
-
     rows = tokens_one.shape[0]
-    mixture = routed(
+    mixture, in_new, out_new = routed(
         tokens_one, routes_one, gates_one, tokens_two, routes_two, gates_two, old_table, new_table,
         gate_up, down_proj)
     tokens = jnp.concatenate([tokens_one, tokens_two], axis=0)
@@ -334,7 +467,7 @@
         lax.all_gather(kv_weight, "grp", axis=1, tiled=True),
         preferred_element_type=F32,
     ).astype(BF)
-    return (out[:rows], projected[:rows], out[rows:], projected[rows:], gate_up_new, down_proj_new)
+    return (out[:rows], projected[:rows], out[rows:], projected[rows:], in_new[None], out_new[None])
 
 
 def solution(mesh):

time: 206 us -> 156 us (0.76); the launches traced: 203 us -> 156 us
  waiting for transfers between devices: 39.8 us -> 0.68 us
  Pallas kernels: 112 us -> 133 us
  starting transfers between devices: 19.9 us -> 0.04 us
  local copies, waits for them, and re-layouts: 12.9 us -> 3 us
    all_to_all x2 -> x0, waiting for transfers between devices: 39.1 us -> none  [the longest x1 39.1 us: local(): lax.all_to_all(pieces, 'ep', split_axis=0, concat_axis=0, tiled=True)]
    pallas_call x1, Pallas kernels: 112 us -> 133 us  [routed(): pl.pallas_call(token_kernel, out_shape=(jax.ShapeDtypeStruct((both, featu...]
    all_to_all x2 -> x0, starting transfers between devices: 19.9 us -> none  [the longest x1 12.8 us: local(): lax.all_to_all(pieces, 'ep', split_axis=0, concat_axis=0, tiled=True)]
    reshape x4 -> x0, local copies, waits for them, and re-layouts: 3.59 us -> none  [the longest x1 1.68 us: local(): gate_up_new = collected[:, :cut].reshape(1, part, 2 * inner)]
    gather x1 -> x0, local copies, waits for them, and re-layouts: 3 us -> none  [local(): spread[sources_new]]
    slice x2 -> x0, local copies, waits for them, and re-layouts: 2.19 us -> none  [the longest x1 1.17 us: local(): gate_up_new = collected[:, :cut].reshape(1, part, 2 * inner)]
    dynamic_slice x2 -> x0, local copies, waits for them, and re-layouts: 2.18 us -> none  [the longest x1 1.17 us: local(): piece_in = lax.dynamic_slice_in_dim(weight_in, start, part, 0)]
  transfers between devices with their start and end apart: 3 -> 1, of which waited for: 1 -> 0; matrix products, arithmetic and copies ran while one was open for 7% -> 2% of each run, Pallas kernels for 55% -> 85%
where the time goes in v3:
time: 156 us
  Pallas kernels  133 us (85%)
  between operations  14.1 us (9%)
  matrix products  3.08 us (2%)
  local copies, waits for them, and re-layouts  3 us (2%)
  other arithmetic  2 us (1%)
    pallas_call x1, Pallas kernels, routed(): pl.pallas_call(token_kernel, out_shape=(jax.ShapeDtypeStruct((both, featu...  133 us
  transfers between devices with their start and end apart: 1, of which 0 were waited for; matrix products, arithmetic and copies ran while one was open for 2% of the time, Pallas kernels for 85%

profile of v3, /device:TPU:1, one launch (start us, length us, event | category | flops | bytes accessed | tf_op | source)
XLA Modules:
  0.0 155.5 jit_solution(17856536172515014439)
XLA Ops:
  7.2 0.0 all-gather.2.cloned.1.call-start
  7.2 0.7 all-gather.2.cloned.1.call-update
  7.9 0.7 convert_element_type.21
  8.6 0.0 copy-start.2
  8.6 0.0 copy-start.3
  8.6 132.6 %routed_tokens.1 = (f32[64,2048]{1,0:T(8,128)}, bf16[256,1408]{1,0:T(8,128)(2,1)}, bf16[704,256]{1,0:T(8,128)(2,1)}) custom-call(bf16[32,2048]{1,0:T(8,128)(2,1)} %t1_ref.1, s32[6,32]{1,0:T(8,128)} %bitcast.11, bf16[6,32]{1,0:T(8,128)(2,1)} %bitcast.13, bf16[32,2048]{1,0:T(8,128)(2,1)} %t2_ref.1, s32[6,32]{1,0:T(8,128)} %bitcast.12, bf16[6,32]{1,0:T(8,128)(2,1)} %bitcast.14, ...), custom_call_target="tpu_custom_call" | custom-call | flops 8000000000 | bytes 200000000 | tf_op jit(solution)/shard_map/routed_tokens/pallas_call | solution.py:391
  141.3 0.0 copy-start
  141.3 0.0 copy-start.1
  141.3 0.0 copy-done.2
  141.3 0.0 copy-done.3
  141.3 1.3 fusion
  142.6 0.7 fusion.6
  143.3 0.0 all-gather.2.cloned.1.call-done
  143.3 3.1 %convolution_convert_fusion = bf16[64,1024]{1,0:T(8,128)(2,1)S(1)} fusion(bf16[2048,1024]{1,0:T(8,128)(2,1)} %all-gather.2.cloned.1.call-done, bf16[64,2048]{1,0:T(8,128)(2,1)S(1)} %get-tuple-element.13, f32[2048]{0:T(1024)S(1)} %convert_element_type.21, f32[64]{0:T(128)S(1)} %add_rsqrt_fusion), kind=kOutput, calls=%fused_computation | convolution fusion | flops 269025280 | bytes 4595968 | tf_op jit(solution)/shard_map/dot_general | solution.py:465
  146.4 0.7 fusion.7
  147.1 0.0 copy-done
  147.1 0.9 copy.20
  147.9 0.0 copy-done.1
  147.9 0.7 copy.21
  (1 shorter events, 0.0 us)
Async XLA Ops:
  7.2 136.2 %all-gather.2.cloned.1.call-start = ((), (), s32[]{:S(2)}) async-start(), calls=%async_computation | async-start | bytes 4718592 | tf_op jit(solution)/shard_map/all_gather | solution.py:467
  8.6 132.7 %copy-start.2 = (bf16[32,2048]{1,0:T(8,128)(2,1)S(1)}, bf16[32,2048]{1,0:T(8,128)(2,1)}, u32[]{:S(2)}) copy-start(bf16[32,2048]{1,0:T(8,128)(2,1)} %t1_ref.1) | copy-start | bytes 393220
  8.6 132.7 %copy-start.3 = (bf16[32,2048]{1,0:T(8,128)(2,1)S(1)}, bf16[32,2048]{1,0:T(8,128)(2,1)}, u32[]{:S(2)}) copy-start(bf16[32,2048]{1,0:T(8,128)(2,1)} %t2_ref.1) | copy-start | bytes 393220
  141.3 5.8 %copy-start = (bf16[256,1408]{1,0:T(8,128)(2,1)S(1)}, bf16[256,1408]{1,0:T(8,128)(2,1)}, u32[]{:S(2)}) copy-start(bf16[256,1408]{1,0:T(8,128)(2,1)} %get-tuple-element.10) | copy-start | bytes 2162692
  141.3 6.7 %copy-start.1 = (bf16[704,256]{1,0:T(8,128)(2,1)S(1)}, bf16[704,256]{1,0:T(8,128)(2,1)}, u32[]{:S(2)}) copy-start(bf16[704,256]{1,0:T(8,128)(2,1)} %get-tuple-element.11) | copy-start | bytes 1081348
Sparse Core Ops, SparseCore 0:
  9.7 122.7 all-gather.1

commit v4 on v3

--- a/solution.py
+++ b/solution.py
@@ -23,12 +23,12 @@
 
 
 def token_kernel(
-    t1_ref, r1_ref, g1_ref, t2_ref, r2_ref, g2_ref, old_ref, new_ref, win_hbm, wout_hbm,
-    o_ref, in_new, out_new,
-    r1v, g1v, r2v, g2v, oldv, newv, srcv, srcs, mid_in, mid_out, pick_in, pick_out, fin_out,
+    t1_ref, r1_ref, g1_ref, t2_ref, r2_ref, g2_ref, old_ref, new_ref, win_hbm, wout_hbm, gain_ref, kv_hbm,
+    o_ref, kv_ref, in_new, out_new,
+    kvw, acc, gainv, r1v, g1v, r2v, g2v, oldv, newv, srcv, srcs, mid_in, mid_out, pick_in, pick_out, fin_out,
     win, wout, ttab, tab, tabs, zbuf, pbuf, abuf, joined, rbuf, cbuf, sbuf, gbuf, own,
     wsem, lsem, tsend, trecv, zsend, zrecv, ysend, yrecv, rsend, rrecv, bsend, brecv,
-    hsend, hrecv, fsend, frecv, selfsem,
+    hsend, hrecv, fsend, frecv, selfsem, ksend, krecv,
 ):
     rows = t1_ref.shape[0]
     both = 2 * rows
@@ -60,6 +60,7 @@
         pltpu.make_async_copy(g2_ref, g2v, lsem.at[3]),
         pltpu.make_async_copy(old_ref, oldv, lsem.at[7]),
         pltpu.make_async_copy(new_ref, newv, lsem.at[8]),
+        pltpu.make_async_copy(gain_ref, gainv, lsem.at[9]),
     ]
     for copy in copies:
         copy.start()
@@ -90,6 +91,12 @@
         return carry
 
     lax.fori_loop(1, 32, greet, 0)
+
+    def greet_grp(off, carry):
+        pl.semaphore_signal(barrier, inc=1, device_id=((grp + off) % 8, ep), device_id_type=MESH)
+        return carry
+
+    lax.fori_loop(1, 8, greet_grp, 0)
 
     for copy in copies:
         copy.wait()
@@ -133,7 +140,7 @@
     for b in range(2):
         for k in range(CHUNKS):
             place_copy(k, b).wait()
-    pl.semaphore_wait(barrier, 35)
+    pl.semaphore_wait(barrier, 42)
 
     def part_in(j):
         return win_hbm.at[0, pl.ds(pl.multiple_of(grp * 256 + j * 8, 8), 8), :]
@@ -232,6 +239,37 @@
     lax.fori_loop(1, 8, start_spread, 0)
     for m in range(3):
         tab_copy(m).wait_recv()
+
+    half = kvw.shape[0] // 2
+    kvw_cols = kv_hbm.shape[1]
+    half_rows = pl.ds(pl.multiple_of(core * half, 8), half)
+    grp_cols = pl.ds(pl.multiple_of(grp * kvw_cols, 128), kvw_cols)
+
+    def kv_copy(off):
+        return pltpu.make_async_remote_copy(
+            src_ref=kv_hbm.at[half_rows, :], dst_ref=kvw.at[half_rows, grp_cols],
+            send_sem=ksend.at[off], recv_sem=krecv.at[off],
+            device_id=((grp + off) % 8, ep), device_id_type=MESH)
+
+    kv_own = pltpu.make_async_copy(kv_hbm.at[half_rows, :], kvw.at[half_rows, grp_cols], selfsem.at[4])
+    kv_swap = pltpu.make_async_remote_copy(
+        src_ref=kvw.at[half_rows, :], dst_ref=kvw.at[half_rows, :], send_sem=ksend.at[0], recv_sem=krecv.at[0],
+        device_id=at_q(y * 2 + 1 - core), device_id_type=MESH)
+
+    def kv_start(off, carry):
+        kv_copy(off).start()
+        return carry
+
+    def kv_wait(off, carry):
+        kv_copy(off).wait_recv()
+        return carry
+
+    def kv_sent(off, carry):
+        kv_copy(off).wait_send()
+        return carry
+
+    kv_own.start()
+    lax.fori_loop(1, 8, kv_start, 0)
 
     total = 8 * slab
     gathered = 4 * both
@@ -301,6 +339,9 @@
 
     lax.fori_loop(0, CHUNKS, expand, 0)
 
+    kv_own.wait()
+    lax.fori_loop(1, 8, kv_wait, 0)
+    kv_swap.start()
     src_copy.wait()
     for copy in own_spread:
         copy.wait()
@@ -335,17 +376,26 @@
 
     lax.fori_loop(0, CHUNKS, combine, 0)
 
-    def finish(k, carry):
+    kv_swap.wait()
+    acc[...] = jnp.zeros_like(acc)
+
+    def finish(k, squares):
         for m in range(3):
             b_copy(k, m).wait_recv()
         sums = own[k]
         for m in range(3):
             sums = sums + gbuf[k, m].astype(F32)
-        o_ref[:, pl.ds(pl.multiple_of(k * width, width), width)] = sums
-        return carry
-
-    lax.fori_loop(0, CHUNKS, finish, 0)
-
+        columns = pl.ds(pl.multiple_of(k * width, width), width)
+        after = (zbuf[k, 0].astype(F32) + sums).astype(BF)
+        o_ref[:, columns] = after
+        values = after.astype(F32)
+        acc[...] += jnp.dot(
+            (values * gainv[:, columns].astype(F32)).astype(BF), kvw[columns, :], preferred_element_type=F32)
+        return squares + jnp.sum(values * values, axis=1, keepdims=True)
+
+    squares = lax.fori_loop(0, CHUNKS, finish, jnp.zeros((both, 1), F32))
+    kv_ref[...] = (acc[...] * lax.rsqrt(squares / (CHUNKS * width) + 1e-06)).astype(BF)
+    lax.fori_loop(1, 8, kv_sent, 0)
     def end_fetch(n, carry):
         for copy in spread_copies(n):
             copy.wait_send()
@@ -376,7 +426,7 @@
     lax.fori_loop(0, CHUNKS, drain, 0)
 
 
-def routed(t1, r1, g1, t2, r2, g2, old_table, new_table, gate_up, down_proj):
+def routed(t1, r1, g1, t2, r2, g2, old_table, new_table, gate_up, down_proj, gain, kv_weight):
     rows, features = t1.shape
     both = 2 * rows
     inner = down_proj.shape[1]
@@ -391,13 +441,17 @@
     return pl.pallas_call(
         token_kernel,
         out_shape=(
-            jax.ShapeDtypeStruct((both, features), F32),
+            jax.ShapeDtypeStruct((both, features), BF),
+            jax.ShapeDtypeStruct((both, 8 * kv_weight.shape[1]), BF),
             jax.ShapeDtypeStruct((part, 2 * inner), BF),
             jax.ShapeDtypeStruct((inner, part), BF),
         ),
-        in_specs=[hbm] * 10,
-        out_specs=(vmem, hbm, vmem),
+        in_specs=[hbm] * 12,
+        out_specs=(vmem, vmem, hbm, vmem),
         scratch_shapes=[
+            pltpu.VMEM((features, 8 * kv_weight.shape[1]), BF),
+            pltpu.VMEM((both, 8 * kv_weight.shape[1]), F32),
+            pltpu.VMEM((1, features), BF),
             pltpu.VMEM((TOP, rows), jnp.int32),
             pltpu.VMEM((TOP, rows), BF),
             pltpu.VMEM((TOP, rows), jnp.int32),
@@ -425,18 +479,19 @@
             pltpu.VMEM((CHUNKS, 3, both, width), BF),
             pltpu.VMEM((CHUNKS, 3, both, width), BF),
             pltpu.VMEM((CHUNKS, both, width), F32),
-            dma((2,)), dma((9,)), dma((3,)), dma((3,)),
+            dma((2,)), dma((10,)), dma((3,)), dma((3,)),
             dma((CHUNKS, 3)), dma((CHUNKS, 3)),
             dma((CHUNKS, 8)), dma((CHUNKS, 8)),
             dma((CHUNKS, 8)), dma((CHUNKS, 8)),
             dma((CHUNKS, 3)), dma((CHUNKS, 3)),
-            dma((2, 32)), dma((2, 32)), dma((2, 32)), dma((2, 32)), dma((4,)),
+            dma((2, 32)), dma((2, 32)), dma((2, 32)), dma((2, 32)), dma((5,)), dma((8,)), dma((8,)),
         ],
         compiler_params=pltpu.CompilerParams(
             collective_id=0, has_side_effects=True, vmem_limit_bytes=60 << 20),
         cost_estimate=pl.CostEstimate(flops=8_000_000_000, bytes_accessed=200_000_000, transcendentals=0),
         name="routed_tokens",
-    )(t1, r1.T, g1.T, t2, r2.T, g2.T, old_table[None, :], new_table[None, :], gate_up, down_proj)
+    )(t1, r1.T, g1.T, t2, r2.T, g2.T, old_table[None, :], new_table[None, :], gate_up, down_proj,
+      gain[None, :], kv_weight)
 
 
 def local(
@@ -454,20 +509,10 @@
     kv_weight,
 ):
     rows = tokens_one.shape[0]
-    mixture, in_new, out_new = routed(
+    hidden, kv, in_new, out_new = routed(
         tokens_one, routes_one, gates_one, tokens_two, routes_two, gates_two, old_table, new_table,
-        gate_up, down_proj)
-    tokens = jnp.concatenate([tokens_one, tokens_two], axis=0)
-    out = (tokens.astype(F32) + mixture).astype(BF)
-    values = out.astype(F32)
-    inverse_rms = lax.rsqrt(jnp.mean(values * values, axis=-1, keepdims=True) + 1e-06)
-    normed = (values * inverse_rms * norm_gain.astype(F32)).astype(BF)
-    projected = jnp.dot(
-        normed,
-        lax.all_gather(kv_weight, "grp", axis=1, tiled=True),
-        preferred_element_type=F32,
-    ).astype(BF)
-    return (out[:rows], projected[:rows], out[rows:], projected[rows:], in_new[None], out_new[None])
+        gate_up, down_proj, norm_gain, kv_weight)
+    return (hidden[:rows], kv[:rows], hidden[rows:], kv[rows:], in_new[None], out_new[None])
 
 
 def solution(mesh):

time: 156 us -> 144 us (0.923)
  the two profiles are of different devices: /device:TPU:1 before, /device:TPU:27 now
where the time goes in v4:
time: 144 us
  Pallas kernels  135 us (94%)
  local copies, waits for them, and re-layouts  8.26 us (6%)
    pallas_call x1, Pallas kernels, routed(): pl.pallas_call(token_kernel, out_shape=(jax.ShapeDtypeStruct((both, featu...  135 us
    unnamed x2, local copies, waits for them, and re-layouts  3.76 us

profile of v4, /device:TPU:27, one launch (start us, length us, event | category | flops | bytes accessed | tf_op | source)
XLA Modules:
  0.0 143.9 jit_solution(3125818150974831057)
XLA Ops:
  0.6 1.3 broadcast_in_dim.17.gain_ref
  1.9 135.0 %routed_tokens.1 = (bf16[64,2048]{1,0:T(8,128)(2,1)}, bf16[64,1024]{1,0:T(8,128)(2,1)}, bf16[256,1408]{1,0:T(8,128)(2,1)}, bf16[704,256]{1,0:T(8,128)(2,1)}) custom-call(bf16[32,2048]{1,0:T(8,128)(2,1)} %t1_ref.1, s32[6,32]{1,0:T(8,128)} %bitcast.10, bf16[6,32]{1,0:T(8,128)(2,1)} %bitcast.12, bf16[32,2048]{1,0:T(8,128)(2,1)} %t2_ref.1, s32[6,32]{1,0:T(8,128)} %bitcast.11, ...), custom_call_target="tpu_custom_call" | custom-call | flops 8000000000 | bytes 200000000 | tf_op jit(solution)/shard_map/routed_tokens/pallas_call | solution.py:441
  137.0 1.7 %fusion = (bf16[32,2048]{1,0:T(8,128)(2,1)}, bf16[32,2048]{1,0:T(8,128)(2,1)}) fusion(bf16[64,2048]{1,0:T(8,128)(2,1)} %get-tuple-element.10), kind=kLoop, calls=%fused_computation | loop fusion | bytes 524288 | tf_op jit(solution)/shard_map/slice | solution.py:515
  138.6 1.5 %fusion.1 = (bf16[32,1024]{1,0:T(8,128)(2,1)}, bf16[32,1024]{1,0:T(8,128)(2,1)}) fusion(bf16[64,1024]{1,0:T(8,128)(2,1)} %get-tuple-element.11), kind=kLoop, calls=%fused_computation.1 | loop fusion | bytes 262144 | tf_op jit(solution)/shard_map/slice | solution.py:515
  140.2 2.0 %copy.20 = bf16[1,256,1408]{2,1,0:T(8,128)(2,1)} copy(bf16[1,256,1408]{2,1,0:T(8,128)(2,1)} %bitcast.8) | data formatting | bytes 1441792
  142.2 1.7 %copy.21 = bf16[1,704,256]{2,1,0:T(8,128)(2,1)} copy(bf16[1,704,256]{2,1,0:T(8,128)(2,1)} %bitcast.9) | data formatting | bytes 720896

commit v5 on v4

--- a/solution.py
+++ b/solution.py
@@ -25,8 +25,8 @@
 def token_kernel(
     t1_ref, r1_ref, g1_ref, t2_ref, r2_ref, g2_ref, old_ref, new_ref, win_hbm, wout_hbm, gain_ref, kv_hbm,
     o_ref, kv_ref, in_new, out_new,
-    kvw, acc, gainv, r1v, g1v, r2v, g2v, oldv, newv, srcv, srcs, mid_in, mid_out, pick_in, pick_out, fin_out,
-    win, wout, ttab, tab, tabs, zbuf, pbuf, abuf, joined, rbuf, cbuf, sbuf, gbuf, own,
+    kvw, acc, gainv, gains, r1v, g1v, r2v, g2v, oldv, newv, srcv, srcs, mid_in, mid_out, pick_in, pick_out, fin_out,
+    win, wout, ttab, tab, tabs, zbuf, pbuf, abuf, joined, rbuf, cbuf, sbuf, gbuf, own, third,
     wsem, lsem, tsend, trecv, zsend, zrecv, ysend, yrecv, rsend, rrecv, bsend, brecv,
     hsend, hrecv, fsend, frecv, selfsem, ksend, krecv,
 ):
@@ -51,7 +51,6 @@
         return (grp, ((q // 2) * 4 + high) * 2 + q % 2)
 
     z_to = (2 * sign, -3 * sign, -sign)
-    z_from = (-2 * sign, -3 * sign, -sign)
 
     copies = [
         pltpu.make_async_copy(r1_ref, r1v, lsem.at[0]),
@@ -100,6 +99,7 @@
 
     for copy in copies:
         copy.wait()
+    gains[...] = gainv[...].astype(F32)
     square = (32, 32)
 
     def named_and_gates(r_ref, g_ref):
@@ -205,8 +205,9 @@
 
     def z_copy(k, m):
         return pltpu.make_async_remote_copy(
-            src_ref=zbuf.at[k, 0], dst_ref=zbuf.at[k, m + 1], send_sem=zsend.at[k, m], recv_sem=zrecv.at[k, m],
-            device_id=at_z(z_to[m]), device_id_type=MESH)
+            src_ref=zbuf.at[k, 3 if m == 1 else 0], dst_ref=zbuf.at[k, m + 1],
+            send_sem=zsend.at[k, m], recv_sem=zrecv.at[k, m],
+            device_id=at_z(-sign if m == 2 else 2 * sign), device_id_type=MESH)
 
     def y_copy(k, off):
         q = (me + off) % 8
@@ -223,15 +224,42 @@
     def b_copy(k, m):
         return pltpu.make_async_remote_copy(
             src_ref=sbuf.at[k, m], dst_ref=gbuf.at[k, m], send_sem=bsend.at[k, m], recv_sem=brecv.at[k, m],
-            device_id=at_z(z_from[m]), device_id_type=MESH)
+            device_id=at_z(-sign if m == 2 else -2 * sign), device_id_type=MESH)
+
+    half = kvw.shape[0] // 2
+    kvw_cols = kv_hbm.shape[1]
+    half_rows = pl.ds(pl.multiple_of(core * half, 8), half)
+
+    def kv_block(g):
+        return kvw.at[half_rows, pl.ds(pl.multiple_of(g * kvw_cols, 128), kvw_cols)]
+
+    def kv_copy(n):
+        other = (grp + 4) % 8
+        target = other if n == 4 else low * 4 + (x + n % 4) % 4
+        return pltpu.make_async_remote_copy(
+            src_ref=kv_block(other) if n > 4 else kv_hbm.at[half_rows, :],
+            dst_ref=kv_block(other) if n > 4 else kv_block(grp),
+            send_sem=ksend.at[n], recv_sem=krecv.at[n], device_id=(target, ep), device_id_type=MESH)
+
+    kv_own = pltpu.make_async_copy(kv_hbm.at[half_rows, :], kv_block(grp), selfsem.at[4])
+    kv_swap = pltpu.make_async_remote_copy(
+        src_ref=kvw.at[half_rows, :], dst_ref=kvw.at[half_rows, :], send_sem=ksend.at[0], recv_sem=krecv.at[0],
+        device_id=at_q(y * 2 + 1 - core), device_id_type=MESH)
 
     for m in range(3):
         tab_copy(m).start()
+    for n in (4, 1, 2, 3):
+        kv_copy(n).start()
+    kv_own.start()
 
     def send_z(k, carry):
-        for m in range(3):
+        for m in (2, 0):
             z_copy(k, m).start()
         return carry
+
+    def hand_on(k):
+        z_copy(k, 2).wait_recv()
+        z_copy(k, 1).start()
 
     lax.fori_loop(0, CHUNKS, send_z, 0)
     for copy in own_spread:
@@ -239,37 +267,6 @@
     lax.fori_loop(1, 8, start_spread, 0)
     for m in range(3):
         tab_copy(m).wait_recv()
-
-    half = kvw.shape[0] // 2
-    kvw_cols = kv_hbm.shape[1]
-    half_rows = pl.ds(pl.multiple_of(core * half, 8), half)
-    grp_cols = pl.ds(pl.multiple_of(grp * kvw_cols, 128), kvw_cols)
-
-    def kv_copy(off):
-        return pltpu.make_async_remote_copy(
-            src_ref=kv_hbm.at[half_rows, :], dst_ref=kvw.at[half_rows, grp_cols],
-            send_sem=ksend.at[off], recv_sem=krecv.at[off],
-            device_id=((grp + off) % 8, ep), device_id_type=MESH)
-
-    kv_own = pltpu.make_async_copy(kv_hbm.at[half_rows, :], kvw.at[half_rows, grp_cols], selfsem.at[4])
-    kv_swap = pltpu.make_async_remote_copy(
-        src_ref=kvw.at[half_rows, :], dst_ref=kvw.at[half_rows, :], send_sem=ksend.at[0], recv_sem=krecv.at[0],
-        device_id=at_q(y * 2 + 1 - core), device_id_type=MESH)
-
-    def kv_start(off, carry):
-        kv_copy(off).start()
-        return carry
-
-    def kv_wait(off, carry):
-        kv_copy(off).wait_recv()
-        return carry
-
-    def kv_sent(off, carry):
-        kv_copy(off).wait_send()
-        return carry
-
-    kv_own.start()
-    lax.fori_loop(1, 8, kv_start, 0)
 
     total = 8 * slab
     gathered = 4 * both
@@ -300,8 +297,18 @@
     mix = jnp.where(
         (found_v == r_col) & (j_col == above(iota((gathered, total), 0), both, 4)), found_g, 0.0).astype(BF)
 
+    kv_copy(4).wait_recv()
+    for n in (5, 6, 7):
+        kv_copy(n).start()
+
+    hand_on(0)
+
     def pack(k, carry):
-        for m in range(3):
+        @pl.when(k + 1 < CHUNKS)
+        def _():
+            hand_on(k + 1)
+
+        for m in range(2):
             z_copy(k, m).wait_recv()
         packed = jnp.dot(pick, zbuf[k].reshape(gathered, width), preferred_element_type=F32)
         pbuf[k] = packed.reshape(8, slab, width).astype(BF)
@@ -340,7 +347,8 @@
     lax.fori_loop(0, CHUNKS, expand, 0)
 
     kv_own.wait()
-    lax.fori_loop(1, 8, kv_wait, 0)
+    for n in (1, 2, 3, 5, 6, 7):
+        kv_copy(n).wait_recv()
     kv_swap.start()
     src_copy.wait()
     for copy in own_spread:
@@ -369,33 +377,47 @@
             r_copy(k, off).wait_recv()
         part = jnp.dot(mix, cbuf[k].reshape(total, width), preferred_element_type=F32)
         own[k] = part[:both]
-        sbuf[k] = part[both:].reshape(3, both, width).astype(BF)
-        for m in range(3):
+        third[k] = part[3 * both:]
+        sbuf[k, 0] = part[both:2 * both].astype(BF)
+        sbuf[k, 1] = part[2 * both:3 * both].astype(BF)
+        for m in (1, 0):
             b_copy(k, m).start()
-        return carry
+
+        @pl.when(k > 0)
+        def _():
+            fold(k - 1)
+
+        return carry
+
+    def fold(k):
+        b_copy(k, 1).wait_recv()
+        sbuf[k, 2] = (third[k] + gbuf[k, 1].astype(F32)).astype(BF)
+        b_copy(k, 2).start()
 
     lax.fori_loop(0, CHUNKS, combine, 0)
+    fold(CHUNKS - 1)
 
     kv_swap.wait()
     acc[...] = jnp.zeros_like(acc)
 
     def finish(k, squares):
-        for m in range(3):
+        for m in (0, 2):
             b_copy(k, m).wait_recv()
-        sums = own[k]
-        for m in range(3):
-            sums = sums + gbuf[k, m].astype(F32)
+        sums = own[k] + gbuf[k, 0].astype(F32) + gbuf[k, 2].astype(F32)
         columns = pl.ds(pl.multiple_of(k * width, width), width)
         after = (zbuf[k, 0].astype(F32) + sums).astype(BF)
         o_ref[:, columns] = after
         values = after.astype(F32)
+        lines = width // 128
+        gain = jnp.concatenate([gains[pl.ds(k * lines + i, 1), :] for i in range(lines)], axis=1)
         acc[...] += jnp.dot(
-            (values * gainv[:, columns].astype(F32)).astype(BF), kvw[columns, :], preferred_element_type=F32)
+            (values * gain).astype(BF), kvw[columns, :], preferred_element_type=F32)
         return squares + jnp.sum(values * values, axis=1, keepdims=True)
 
     squares = lax.fori_loop(0, CHUNKS, finish, jnp.zeros((both, 1), F32))
     kv_ref[...] = (acc[...] * lax.rsqrt(squares / (CHUNKS * width) + 1e-06)).astype(BF)
-    lax.fori_loop(1, 8, kv_sent, 0)
+    for n in range(1, 8):
+        kv_copy(n).wait_send()
     def end_fetch(n, carry):
         for copy in spread_copies(n):
             copy.wait_send()
@@ -451,7 +473,8 @@
         scratch_shapes=[
             pltpu.VMEM((features, 8 * kv_weight.shape[1]), BF),
             pltpu.VMEM((both, 8 * kv_weight.shape[1]), F32),
-            pltpu.VMEM((1, features), BF),
+            pltpu.VMEM((features // 128, 128), BF),
+            pltpu.VMEM((features // 128, 128), F32),
             pltpu.VMEM((TOP, rows), jnp.int32),
             pltpu.VMEM((TOP, rows), BF),
             pltpu.VMEM((TOP, rows), jnp.int32),
@@ -479,6 +502,7 @@
             pltpu.VMEM((CHUNKS, 3, both, width), BF),
             pltpu.VMEM((CHUNKS, 3, both, width), BF),
             pltpu.VMEM((CHUNKS, both, width), F32),
+            pltpu.VMEM((CHUNKS, both, width), F32),
             dma((2,)), dma((10,)), dma((3,)), dma((3,)),
             dma((CHUNKS, 3)), dma((CHUNKS, 3)),
             dma((CHUNKS, 8)), dma((CHUNKS, 8)),
@@ -491,7 +515,31 @@
         cost_estimate=pl.CostEstimate(flops=8_000_000_000, bytes_accessed=200_000_000, transcendentals=0),
         name="routed_tokens",
     )(t1, r1.T, g1.T, t2, r2.T, g2.T, old_table[None, :], new_table[None, :], gate_up, down_proj,
-      gain[None, :], kv_weight)
+      gain.reshape(features // 128, 128), kv_weight)
+
+
+def hand_out(hid_ref, kv_ref, in_ref, out_ref, h1_ref, k1_ref, h2_ref, k2_ref, in_new, out_new, hid, kv, inv, outv, sems):
+    rows = h1_ref.shape[0]
+    first, second = pl.ds(0, rows), pl.ds(rows, rows)
+    reads = [
+        pltpu.make_async_copy(src, dst, sems.at[i])
+        for i, (src, dst) in enumerate(((in_ref, inv), (out_ref, outv), (hid_ref, hid), (kv_ref, kv)))
+    ]
+    writes = [
+        [(inv, in_new.at[0])], [(outv, out_new.at[0])],
+        [(hid.at[first], h1_ref), (hid.at[second], h2_ref)], [(kv.at[first], k1_ref), (kv.at[second], k2_ref)],
+    ]
+    for copy in reads:
+        copy.start()
+    started = []
+    for copy, targets in zip(reads, writes):
+        copy.wait()
+        for src, dst in targets:
+            write = pltpu.make_async_copy(src, dst, sems.at[4 + len(started)])
+            write.start()
+            started.append(write)
+    for write in started:
+        write.wait()
 
 
 def local(
@@ -512,7 +560,21 @@
     hidden, kv, in_new, out_new = routed(
         tokens_one, routes_one, gates_one, tokens_two, routes_two, gates_two, old_table, new_table,
         gate_up, down_proj, norm_gain, kv_weight)
-    return (hidden[:rows], kv[:rows], hidden[rows:], kv[rows:], in_new[None], out_new[None])
+    hbm = pl.BlockSpec(memory_space=pltpu.HBM)
+    token_rows = jax.ShapeDtypeStruct((rows, hidden.shape[1]), BF)
+    kv_rows = jax.ShapeDtypeStruct((rows, kv.shape[1]), BF)
+    return pl.pallas_call(
+        hand_out,
+        out_shape=(
+            token_rows, kv_rows, token_rows, kv_rows,
+            jax.ShapeDtypeStruct((1,) + in_new.shape, BF), jax.ShapeDtypeStruct((1,) + out_new.shape, BF)),
+        in_specs=[hbm] * 4,
+        out_specs=(hbm,) * 6,
+        scratch_shapes=[pltpu.VMEM(array.shape, BF) for array in (hidden, kv, in_new, out_new)]
+        + [pltpu.SemaphoreType.DMA((10,))],
+        compiler_params=pltpu.CompilerParams(vmem_limit_bytes=60 << 20),
+        name="hand_out",
+    )(hidden, kv, in_new, out_new)
 
 
 def solution(mesh):

time: 144 us -> 121 us (0.84)
  the two profiles are of different devices: /device:TPU:27 before, /device:TPU:1 now
where the time goes in v5:
time: 121 us; the launch traced here: 120 us
  Pallas kernels  119 us (98%)
    pallas_call x1, Pallas kernels, routed(): pl.pallas_call(token_kernel, out_shape=(jax.ShapeDtypeStruct((both, featu...  117 us

profile of v5, /device:TPU:1, one launch (start us, length us, event | category | flops | bytes accessed | tf_op | source)
XLA Modules:
  0.0 119.9 jit_solution(3319916193269267560)
XLA Ops:
  0.6 117.0 %routed_tokens.1 = (bf16[64,2048]{1,0:T(8,128)(2,1)}, bf16[64,1024]{1,0:T(8,128)(2,1)}, bf16[256,1408]{1,0:T(8,128)(2,1)}, bf16[704,256]{1,0:T(8,128)(2,1)}) custom-call(bf16[32,2048]{1,0:T(8,128)(2,1)} %t1_ref.1, s32[6,32]{1,0:T(8,128)} %bitcast.7, bf16[6,32]{1,0:T(8,128)(2,1)} %bitcast.10, bf16[32,2048]{1,0:T(8,128)(2,1)} %t2_ref.1, s32[6,32]{1,0:T(8,128)} %bitcast.8, ...), custom_call_target="tpu_custom_call" | custom-call | flops 8000000000 | bytes 200000000 | tf_op jit(solution)/shard_map/routed_tokens/pallas_call | solution.py:463
  117.6 2.3 %hand_out.1 = (bf16[32,2048]{1,0:T(8,128)(2,1)}, bf16[32,1024]{1,0:T(8,128)(2,1)}, bf16[32,2048]{1,0:T(8,128)(2,1)}, bf16[32,1024]{1,0:T(8,128)(2,1)}, bf16[1,25...) custom-call(bf16[64,2048]{1,0:T(8,128)(2,1)} %get-tuple-element.10.hid_ref, ...), custom_call_target="tpu_custom_call" | custom-call | tf_op jit(solution)/shard_map/hand_out/pallas_call | solution.py:566

commit v6 on v5

--- a/solution.py
+++ b/solution.py
@@ -155,7 +155,7 @@
         return (((y + dy) % 4) * 4 + (high + dz) % 4) * 2 + (core + dc) % 2
 
     def ep_at(n, back):
-        dy, dz, dc = (n // 2) % 4, n // 8, n % 2
+        dy, dz, dc = n // 8, n % 4, (n // 4) % 2
         if back:
             return ep_of(4 - dy, 4 - dz, dc)
         return ep_of(dy, dz, dc)
@@ -264,7 +264,7 @@
     lax.fori_loop(0, CHUNKS, send_z, 0)
     for copy in own_spread:
         copy.start()
-    lax.fori_loop(1, 8, start_spread, 0)
+    lax.fori_loop(1, 8, lambda n, carry: start_spread(n * 4, carry), 0)
     for m in range(3):
         tab_copy(m).wait_recv()
 
@@ -312,13 +312,14 @@
             z_copy(k, m).wait_recv()
         packed = jnp.dot(pick, zbuf[k].reshape(gathered, width), preferred_element_type=F32)
         pbuf[k] = packed.reshape(8, slab, width).astype(BF)
-        for off in range(1, 8):
+        for off in (2, 6, 4, 3, 7, 5, 1):
             y_copy(k, off).start()
         abuf[k, me] = pbuf[k, me]
         return carry
 
-    lax.fori_loop(0, CHUNKS, pack, 0)
-    lax.fori_loop(8, 32, start_spread, 0)
+    lax.fori_loop(0, CHUNKS - 1, pack, 0)
+    lax.fori_loop(0, 24, lambda i, carry: start_spread((i // 3) * 4 + i % 3 + 1, carry), 0)
+    lax.fori_loop(CHUNKS - 1, CHUNKS, pack, 0)
     win_copy.wait()
     joined[...] = jnp.zeros_like(joined)
 
@@ -339,7 +340,7 @@
         result = jnp.dot(
             hidden, wout[:, pl.ds(pl.multiple_of(k * width, width), width)], preferred_element_type=F32)
         rbuf[k] = result.reshape(8, slab, width).astype(BF)
-        for off in range(1, 8):
+        for off in (2, 6, 4, 3, 7, 5, 1):
             r_copy(k, off).start()
         cbuf[k, me] = rbuf[k, me]
         return carry

time: 121 us -> 119 us (0.983)
    pallas_call x1, Pallas kernels: 117 us -> 116 us  [routed(): pl.pallas_call(token_kernel, out_shape=(jax.ShapeDtypeStruct((both, featu...]
where the time goes in v6:
time: 119 us
  Pallas kernels  118 us (99%)
    pallas_call x1, Pallas kernels, routed(): pl.pallas_call(token_kernel, out_shape=(jax.ShapeDtypeStruct((both, featu...  116 us

profile of v6, /device:TPU:1, one launch (start us, length us, event | category | flops | bytes accessed | tf_op | source)
XLA Modules:
  0.0 118.5 jit_solution(9674652702735710095)
XLA Ops:
  0.6 115.6 %routed_tokens.1 = (bf16[64,2048]{1,0:T(8,128)(2,1)}, bf16[64,1024]{1,0:T(8,128)(2,1)}, bf16[256,1408]{1,0:T(8,128)(2,1)}, bf16[704,256]{1,0:T(8,128)(2,1)}) custom-call(bf16[32,2048]{1,0:T(8,128)(2,1)} %t1_ref.1, s32[6,32]{1,0:T(8,128)} %bitcast.7, bf16[6,32]{1,0:T(8,128)(2,1)} %bitcast.10, bf16[32,2048]{1,0:T(8,128)(2,1)} %t2_ref.1, s32[6,32]{1,0:T(8,128)} %bitcast.8, ...), custom_call_target="tpu_custom_call" | custom-call | flops 8000000000 | bytes 200000000 | tf_op jit(solution)/shard_map/routed_tokens/pallas_call | solution.py:464
  116.2 2.3 %hand_out.1 = (bf16[32,2048]{1,0:T(8,128)(2,1)}, bf16[32,1024]{1,0:T(8,128)(2,1)}, bf16[32,2048]{1,0:T(8,128)(2,1)}, bf16[32,1024]{1,0:T(8,128)(2,1)}, bf16[1,25...) custom-call(bf16[64,2048]{1,0:T(8,128)(2,1)} %get-tuple-element.10.hid_ref, ...), custom_call_target="tpu_custom_call" | custom-call | tf_op jit(solution)/shard_map/hand_out/pallas_call | solution.py:567
